TPU v7x, 512 devices: a whole 4x4x16 slice. The times are simulated.
512 devices in a mesh: prefix: 64 (over z, x), tensor: 8 (over y, core).
Axes of the slice: x: 4, y: 4, z: 16, core: 2. Of those that a mesh axis runs over, the one named last changes fastest.
Arguments:
- queries: bfloat16 [4096, 8192], P(('prefix', 'tensor')), may hold values from -24 to 24
- suffix_kv: bfloat16 [4096, 2, 8, 64, 128], P('prefix', None, 'tensor'), may hold values from -15 to 15
- suffix_lengths: int32 [4096], P('prefix'), may hold values from 1 to 64
- prefix_kv: bfloat16 [64, 2, 8, 4096, 128], P('prefix', None, 'tensor'), may hold values from -16 to 16
- tree_ids: int32 [4096], P('prefix'), may hold values from 0 to 63, as said below
- owner_map: int32 [64], replicated, may hold values from 0 to 63, as said below
Outputs:
- attended: bfloat16 [4096, 8192], P(('prefix', 'tensor'))
Inputs may be any that keep to these rules, and one draw needn't show every extreme that they name: `tree_ids`: in each aligned block of 64 rows (the rows of one index of prefix) no prompt is named by more than 2 rows, and some prompt is named by exactly 2 rows in every block. `owner_map`: A permutation: every row of prefix_kv holds the prefix of exactly one prompt.
All inputs are finite; a program needn't handle non-finite values.
Results may differ from a plain program's by a relative error of at most 0.0017.
Values may be sent and summed in bfloat16 or wider, within the bound.
No kernel may reach another device: no remote copies, remote signals or barrier semaphores. Data moves between devices by JAX's collectives and lax.ppermute only.
A program may use at most 64 MiB of HBM per device.

v0:
```python
import math

import jax
import jax.numpy as jnp
from jax import lax
from jax.sharding import PartitionSpec as P

H = 64
KVH = 8
HD = 128


def prefix_attend(slot_block, key_rows, value_rows):
    sources, slot_count, row_width = slot_block.shape
    kv_heads = key_rows.shape[0]
    group_size = row_width // (kv_heads * HD)
    per_source = slot_count * (row_width // HD)
    pieces = math.gcd(sources, max(1, sources * per_source // 512))
    shaped = slot_block.reshape(pieces, sources // pieces, slot_count, kv_heads, group_size, HD)
    score_scale = 1.0 / math.sqrt(HD)

    def attend_piece(query_piece):
        scores = (
            jnp.einsum(
                "skgid,gnd->skgin", query_piece, key_rows, preferred_element_type=jnp.float32
            )
            * score_scale
        )
        row_top = jnp.max(scores, axis=-1)
        weights = jnp.exp(scores - row_top[..., None])
        mass_sum = jnp.sum(weights, axis=-1)
        weighted = jnp.einsum(
            "skgin,gnd->skgid",
            weights.astype(jnp.bfloat16),
            value_rows,
            preferred_element_type=jnp.float32,
        )
        return (weighted / mass_sum[..., None], row_top, mass_sum)

    prefix_part, prefix_top, prefix_total = lax.map(attend_piece, shaped)
    head_count = row_width // HD
    return (
        prefix_part.reshape(sources, slot_count, row_width),
        prefix_top.reshape(sources, slot_count, head_count),
        prefix_total.reshape(sources, slot_count, head_count),
    )


def on_device(queries, suffix_kv, suffix_lengths, prefix_kv, tree_ids, owner_map):
    owners = lax.axis_size("prefix")
    head_groups = lax.axis_size("tensor")
    kv_local = KVH // head_groups
    group_size = H // KVH
    row_width = H // head_groups * HD
    score_scale = 1.0 / math.sqrt(HD)
    local_q = lax.all_to_all(queries, "tensor", split_axis=1, concat_axis=0, tiled=True)
    rows_home = local_q.shape[0]
    capacity = max(2, 2 * rows_home // owners)
    prompts = owner_map.shape[0]
    prompt_iota = jnp.arange(prompts, dtype=jnp.int32)
    prompt_match = tree_ids[:, None] == prompt_iota[None, :]
    owner_row = jnp.sum(jnp.where(prompt_match, owner_map[None, :], 0), axis=1)
    row_iota = jnp.arange(rows_home, dtype=jnp.int32)
    earlier = (tree_ids[:, None] == tree_ids[None, :]) & (row_iota[None, :] < row_iota[:, None])
    slot_rank = jnp.sum(earlier.astype(jnp.int32), axis=1)
    owner_iota = jnp.arange(owners, dtype=jnp.int32)
    slot_iota = jnp.arange(capacity, dtype=jnp.int32)
    placed = (owner_row[None, None, :] == owner_iota[:, None, None]) & (
        slot_rank[None, None, :] == slot_iota[None, :, None]
    )
    key_rows = prefix_kv[0, 0]
    value_rows = prefix_kv[0, 1]
    outgoing = jnp.einsum(
        "ojr,rc->ojc", placed.astype(jnp.bfloat16), local_q, preferred_element_type=jnp.float32
    ).astype(jnp.bfloat16)
    part_slots, top_slots, total_slots = prefix_attend(
        lax.all_to_all(outgoing, "prefix", split_axis=0, concat_axis=0, tiled=True),
        key_rows,
        value_rows,
    )
    returned = (
        lax.all_to_all(part_slots, "prefix", split_axis=0, concat_axis=0, tiled=True),
        lax.all_to_all(top_slots, "prefix", split_axis=0, concat_axis=0, tiled=True),
        lax.all_to_all(total_slots, "prefix", split_axis=0, concat_axis=0, tiled=True),
    )
    back_part, back_top, back_total = returned
    picker = placed.astype(jnp.float32)
    prefix_part = jnp.einsum("ojr,ojc->rc", picker, back_part, precision=lax.Precision.HIGHEST)
    prefix_top = jnp.einsum("ojr,ojh->rh", picker, back_top, precision=lax.Precision.HIGHEST)
    prefix_total = jnp.einsum("ojr,ojh->rh", picker, back_total, precision=lax.Precision.HIGHEST)
    prefix_part = prefix_part.reshape(rows_home, kv_local, group_size, HD)
    prefix_top = prefix_top.reshape(rows_home, kv_local, group_size)
    prefix_total = prefix_total.reshape(rows_home, kv_local, group_size)
    query_home = local_q.reshape(rows_home, kv_local, group_size, HD)
    suffix_scores = (
        jnp.einsum(
            "rgid,rgnd->rgin", query_home, suffix_kv[:, 0], preferred_element_type=jnp.float32
        )
        * score_scale
    )
    position = jnp.arange(suffix_kv.shape[3], dtype=jnp.int32)
    is_live = (position[None, :] < suffix_lengths[:, None])[:, None, None, :]
    suffix_top = jnp.max(jnp.where(is_live, suffix_scores, -jnp.inf), axis=-1)
    suffix_weights = jnp.where(is_live, jnp.exp(suffix_scores - suffix_top[..., None]), 0.0)
    suffix_total = jnp.sum(suffix_weights, axis=-1)
    suffix_sum = jnp.einsum(
        "rgin,rgnd->rgid",
        suffix_weights.astype(jnp.bfloat16),
        suffix_kv[:, 1],
        preferred_element_type=jnp.float32,
    )
    joint_top = jnp.maximum(prefix_top, suffix_top)
    prefix_mass = prefix_total * jnp.exp(prefix_top - joint_top)
    suffix_mass = jnp.exp(suffix_top - joint_top)
    attended = (prefix_mass[..., None] * prefix_part + suffix_mass[..., None] * suffix_sum) / (
        prefix_mass + suffix_mass * suffix_total
    )[..., None]
    attended = attended.reshape(rows_home, row_width).astype(jnp.bfloat16)
    return lax.all_to_all(attended, "tensor", split_axis=0, concat_axis=1, tiled=True)


def solution(mesh):
    in_specs = (
        P(("prefix", "tensor"), None),
        P("prefix", None, "tensor", None, None),
        P("prefix"),
        P("prefix", None, "tensor", None, None),
        P("prefix"),
        P(),
    )
    out_specs = P(("prefix", "tensor"), None)
    return jax.shard_map(
        on_device, mesh=mesh, in_specs=in_specs, out_specs=out_specs, check_vma=False
    )
```

profile of v0, /device:TPU:1, one launch (start us, length us, event | category | flops | bytes accessed | tf_op | source)
XLA Modules:
  0.0 149.2 jit_solution(4013298292729371955)
XLA Ops:
  0.0 10.1 %all-to-all-start = ((bf16[8,8,1024]{2,0,1:T(8,128)(2,1)}), bf16[8,8,1024]{2,0,1:T(8,128)(2,1)S(1)}, u32[]{:S(2)}, u32[]{:S(2)}) async-start(bf16[8,8,1024]{2,0,1:T(8,128)(2,1)} %bitcast.149), calls=%async_computation | async-start | bytes 262144 | tf_op jit(solution)/shard_map/all_to_all | solution.py:56
  10.1 0.9 select_reduce_fusion.1
  11.0 0.1 iota_compare_fusion.2
  11.1 4.3 %all-to-all-done = bf16[8,8,1024]{2,0,1:T(8,128)(2,1)S(1)} async-done(((bf16[8,8,1024]{2,0,1:T(8,128)(2,1)}), bf16[8,8,1024]{2,0,1:T(8,128)(2,1)S(1)}, u32[]{:S(2)}, u32[]{:S(2)}) %all-to-all-start) | async-done | bytes 131104 | tf_op jit(solution)/shard_map/all_to_all | solution.py:56
  15.4 0.3 convolution_convert_fusion
  15.7 1.0 copy.37
  16.7 14.1 %all-to-all-start.1 = ((bf16[64,2,1024]{2,1,0:T(2,128)(2,1)}), bf16[64,2,1024]{2,1,0:T(2,128)(2,1)S(1)}, u32[]{:S(2)}, u32[]{:S(2)}) async-start(bf16[64,2,1024]{2,1,0:T(2,128)(2,1)} %copy.37), calls=%async_computation.1 | async-start | bytes 524288 | tf_op jit(solution)/shard_map/all_to_all | solution.py:77
  30.8 1.7 %slice_bitcast_fusion = (bf16[1,4096,128]{2,1,0:T(8,128)(2,1)S(1)}, bf16[1,4096,128]{2,1,0:T(8,128)(2,1)S(1)}) fusion(bf16[1,2,1,4096,128]{4,3,2,1,0:T(8,128)(2,1)} %param.11), kind=kLoop, calls=%fused_computation.34 | loop fusion | bytes 4194304 | tf_op jit(solution)/shard_map/squeeze | solution.py:72
  32.5 17.7 %all-to-all-done.1 = bf16[64,2,1024]{2,1,0:T(2,128)(2,1)S(1)} async-done(((bf16[64,2,1024]{2,1,0:T(2,128)(2,1)}), bf16[64,2,1024]{2,1,0:T(2,128)(2,1)S(1)}, u32[]{:S(2)}, u32[]{:S(2)}) %all-to-all-start.1) | async-done | bytes 262176 | tf_op jit(solution)/shard_map/all_to_all | solution.py:77
  50.2 0.2 reshape.185
  50.4 0.0 copy-start
  50.4 10.0 %while.14 = (s32[]{:T(128)}, f32[2,32,2,1,8,128]{5,4,2,1,3,0:T(8,128)S(1)}, f32[2,32,2,1,8]{4,2,1,3,0:T(2,128)S(1)}, f32[2,32,2,1,8]{4,2,1,3,0:T(2,128)}, bf16[2...) while((s32[]{:T(128)}, ...), condition=%wide.region_5.6_spmd, body=%wide.region_2.5_spmd.sunk | while | flops 1090583552 | bytes 27859548 | solution.py:40
  50.4 1.4 bitcast_reduce_fusion.2
  51.8 1.5 %fusion.67 = f32[32,2,8]{2,1,0:T(2,128)S(1)} fusion(f32[32,2,8,4096]{3,2,1,0:T(8,128)S(1)} %get-tuple-element.142, f32[32,2,8]{2,1,0:T(2,128)S(1)} %get-tuple-element.143), kind=kLoop, calls=%fused_computation.3.clone.1 | loop fusion | flops 6290944 | bytes 8392704 | tf_op jit(solution)/shard_map/while/body/eval_jaxpr/reduce_sum | solution.py:31
  53.3 0.6 bitcast_dynamic-update-slice_fusion.3
  53.9 1.5 fusion.68
  55.4 1.4 bitcast_reduce_fusion.2
  56.8 1.5 %fusion.67 = f32[32,2,8]{2,1,0:T(2,128)S(1)} fusion(f32[32,2,8,4096]{3,2,1,0:T(8,128)S(1)} %get-tuple-element.142, f32[32,2,8]{2,1,0:T(2,128)S(1)} %get-tuple-element.143), kind=kLoop, calls=%fused_computation.3.clone.1 | loop fusion | flops 6290944 | bytes 8392704 | tf_op jit(solution)/shard_map/while/body/eval_jaxpr/reduce_sum | solution.py:31
  58.3 0.6 bitcast_dynamic-update-slice_fusion.3
  58.9 1.5 fusion.68
  60.4 21.0 %all_to_all.55 = f32[64,2,8]{2,1,0:T(2,128)S(1)} all-to-all(f32[64,2,8]{2,1,0:T(2,128)S(1)} %bitcast.150), channel_id=1, replica_groups=mesh['prefix'=64,'tensor'=8] {'prefix'}, dimensions={0} | all-to-all | bytes 8192 | tf_op jit(solution)/shard_map/all_to_all | solution.py:83
  81.4 4.6 %all-to-all-start.2 = ((f32[64,2,8]{2,1,0:T(2,128)}), f32[64,2,8]{2,1,0:T(2,128)S(1)}, u32[]{:S(2)}, u32[]{:S(2)}) async-start(f32[64,2,8]{2,1,0:T(2,128)} %bitcast.26), calls=%async_computation.2 | async-start | bytes 131072 | tf_op jit(solution)/shard_map/all_to_all | solution.py:84
  86.0 1.0 reshape.190
  87.1 13.0 %all-to-all-done.2 = f32[64,2,8]{2,1,0:T(2,128)S(1)} async-done(((f32[64,2,8]{2,1,0:T(2,128)}), f32[64,2,8]{2,1,0:T(2,128)S(1)}, u32[]{:S(2)}, u32[]{:S(2)}) %all-to-all-start.2) | async-done | bytes 4128 | tf_op jit(solution)/shard_map/all_to_all | solution.py:84
  100.1 4.6 %all-to-all-start.4 = ((f32[64,2,1024]{2,1,0:T(2,128)}), f32[64,2,1024]{2,1,0:T(2,128)S(1)}, u32[]{:S(2)}, u32[]{:S(2)}) async-start(f32[64,2,1024]{2,1,0:T(2,128)} %reshape.190), calls=%async_computation.4 | async-start | bytes 1048576 | tf_op jit(solution)/shard_map/all_to_all | solution.py:82
  104.7 0.0 copy-done
  104.7 0.1 iota_compare_fusion
  104.8 2.0 %select_reduce_fusion = (f32[64,8]{1,0:T(8,128)S(1)}, f32[64,8,64]{2,1,0:T(8,128)S(1)}) fusion(pred[64,64]{1,0:T(8,128)(4,1)S(1)} %iota_compare_fusion, bf16[64,8,128]{2,1,0:T(8,128)(2,1)S(1)} %bitcast.147, bf16[64,2,1,64,128]{4,3,2,1,0:T(8,128)(2,1)} %param.9), kind=kOutput, calls=%fused_computation.39 | convolution fusion | flops 8486400 | bytes 1316864 | tf_op jit(solution)/shard_map/rgid,rgnd->rgin/dot_general | solution.py:96
  106.8 0.1 copy.44
  106.8 0.2 fusion.34
  107.1 0.1 copy.50
  107.1 0.3 convolution_bitcast_fusion.1
  107.4 0.3 multiply_add_fusion
  107.7 0.1 copy.45
  107.7 0.1 copy.48
  107.8 0.1 copy.51
  107.9 24.4 %all-to-all-done.4 = f32[64,2,1024]{2,1,0:T(2,128)S(1)} async-done(((f32[64,2,1024]{2,1,0:T(2,128)}), f32[64,2,1024]{2,1,0:T(2,128)S(1)}, u32[]{:S(2)}, u32[]{:S(2)}) %all-to-all-start.4) | async-done | bytes 524320 | tf_op jit(solution)/shard_map/all_to_all | solution.py:82
  132.3 0.5 convolution_bitcast_fusion
  132.9 0.1 bitcast_multiply_fusion
  133.0 1.7 %fusion.27 = bf16[64,8,128]{2,1,0:T(8,128)(2,1)S(1)} fusion(f32[64,8,128]{2,1,0:T(8,128)S(1)} %bitcast_multiply_fusion, bf16[64,2,1,64,128]{4,3,2,1,0:T(8,128)(2,1)} %param.9, f32[64,8,64]{2,1,0:T(8,128)S(1)} %get-tuple-element.93, f32[64,8]{1,0:T(8,128)S(1)} %copy.51, f32[64,8]{1,0:T(8,128)S(1)} %get-tuple-element.92, f32[64,8]{1,0:T(8,128)S(1)} %copy.48, ...), kind=kOutput, calls=%fused_computation.26 | convolution fusion | flops 8749056 | bytes 1583104 | tf_op jit(solution)/shard_map/rgin,rgnd->rgid/dot_general | solution.py:106
  134.8 0.1 convert_element_type.26
  134.8 13.8 %all_to_all.56 = bf16[8,8,1024]{2,1,0:T(8,128)(2,1)S(1)} all-to-all(bf16[8,8,1024]{2,1,0:T(8,128)(2,1)S(1)} %convert_element_type.26), channel_id=1, replica_groups=mesh['prefix'=64,'tensor'=8] {'tensor'}, dimensions={0} | all-to-all | bytes 262144 | tf_op jit(solution)/shard_map/all_to_all | solution.py:119
  148.6 0.7 copy.87
  (6 shorter events, 0.1 us)
Async XLA Ops:
  0.0 15.4 %all-to-all-start = ((bf16[8,8,1024]{2,0,1:T(8,128)(2,1)}), bf16[8,8,1024]{2,0,1:T(8,128)(2,1)S(1)}, u32[]{:S(2)}, u32[]{:S(2)}) async-start(bf16[8,8,1024]{2,0,1:T(8,128)(2,1)} %bitcast.149), calls=%async_computation | async-start | bytes 262144 | tf_op jit(solution)/shard_map/all_to_all | solution.py:56
  16.7 33.5 %all-to-all-start.1 = ((bf16[64,2,1024]{2,1,0:T(2,128)(2,1)}), bf16[64,2,1024]{2,1,0:T(2,128)(2,1)S(1)}, u32[]{:S(2)}, u32[]{:S(2)}) async-start(bf16[64,2,1024]{2,1,0:T(2,128)(2,1)} %copy.37), calls=%async_computation.1 | async-start | bytes 524288 | tf_op jit(solution)/shard_map/all_to_all | solution.py:77
  50.4 54.3 %copy-start = (s32[64]{0:T(128)S(1)}, s32[64]{0:T(128)}, u32[]{:S(2)}) copy-start(s32[64]{0:T(128)} %param.10) | copy-start | bytes 772
  81.4 18.6 %all-to-all-start.2 = ((f32[64,2,8]{2,1,0:T(2,128)}), f32[64,2,8]{2,1,0:T(2,128)S(1)}, u32[]{:S(2)}, u32[]{:S(2)}) async-start(f32[64,2,8]{2,1,0:T(2,128)} %bitcast.26), calls=%async_computation.2 | async-start | bytes 131072 | tf_op jit(solution)/shard_map/all_to_all | solution.py:84
  100.1 32.3 %all-to-all-start.4 = ((f32[64,2,1024]{2,1,0:T(2,128)}), f32[64,2,1024]{2,1,0:T(2,128)S(1)}, u32[]{:S(2)}, u32[]{:S(2)}) async-start(f32[64,2,1024]{2,1,0:T(2,128)} %reshape.190), calls=%async_computation.4 | async-start | bytes 1048576 | tf_op jit(solution)/shard_map/all_to_all | solution.py:82
where the time goes:
time: 150 us; the launch traced here: 149 us
  waiting for transfers between devices  59.3 us (40%)
  blocking collectives  34.8 us (23%)
  starting transfers between devices  33.5 us (22%)
  matrix products  10.7 us (7%)
  local copies, waits for them, and re-layouts  6.28 us (4%)
  other arithmetic  4.47 us (3%)
    all_to_all x1, waiting for transfers between devices, on_device(): lax.all_to_all(part_slots, 'prefix', split_axis=0, concat_axis=0, tiled=T...  24.4 us
    all_to_all x1, blocking collectives, on_device(): lax.all_to_all(top_slots, 'prefix', split_axis=0, concat_axis=0, tiled=True)  21 us
    all_to_all x1, waiting for transfers between devices, on_device(): lax.all_to_all(outgoing, 'prefix', split_axis=0, concat_axis=0, tiled=True)  17.7 us
    all_to_all x1, starting transfers between devices, on_device(): lax.all_to_all(outgoing, 'prefix', split_axis=0, concat_axis=0, tiled=True)  14.1 us
    all_to_all x1, blocking collectives, on_device(): lax.all_to_all(attended, 'tensor', split_axis=0, concat_axis=1, tiled=True)  13.8 us
    all_to_all x1, waiting for transfers between devices, on_device(): lax.all_to_all(total_slots, 'prefix', split_axis=0, concat_axis=0, tiled=...  13 us
    all_to_all x1, starting transfers between devices, on_device(): lax.all_to_all(queries, 'tensor', split_axis=1, concat_axis=0, tiled=True)  10.1 us
    all_to_all x1, starting transfers between devices, on_device(): lax.all_to_all(part_slots, 'prefix', split_axis=0, concat_axis=0, tiled=T...  4.63 us
  transfers between devices with their start and end apart: 4, of which 4 were waited for; matrix products, arithmetic and copies ran while one was open for 5% of the time, Pallas kernels for 0%

commit v1 on v0

v1 whole, which is shorter than its diff:
```python
import math

import jax
import jax.numpy as jnp
from jax import lax
from jax.experimental import pallas as pl
from jax.experimental.pallas import tpu as pltpu
from jax.sharding import PartitionSpec as P

H = 64
KVH = 8
HD = 128
GROUP = H // KVH
SLOTS = 2
CODE_TOP = 32767.0
SCORE_SCALE = math.log2(math.e) / math.sqrt(HD)

BLOCK = 128
CHUNK = 512

NT = (((1,), (1,)), ((), ()))


def dispatch_kernel(slot_ref, q_ref, out_ref, home_ref, tile_ref):
    tensor, rows, width = q_ref.shape
    for t in range(tensor):
        for h in range(GROUP):
            tile_ref[pl.ds((t * GROUP + h) * rows, rows), :] = q_ref[
                t, :, h * HD : (h + 1) * HD
            ].astype(jnp.float32)
    for r in range(0, tensor * rows, 2):
        pair = []
        for k in range(2):
            t, i = divmod(r + k, rows)
            tile = tile_ref[pl.ds(t * GROUP * rows + i, GROUP, stride=rows), :]
            pair.append(tile)
            out_ref[slot_ref[r + k]] = tile.astype(jnp.bfloat16)
        home_ref[r // 2] = jnp.concatenate(pair, axis=0).astype(jnp.bfloat16)


def dispatch(slot, q_rows):
    tensor, rows, width = q_rows.shape
    count = tensor * rows
    owners = count
    return pl.pallas_call(
        dispatch_kernel,
        out_shape=(
            jax.ShapeDtypeStruct((owners * SLOTS, GROUP, HD), jnp.bfloat16),
            jax.ShapeDtypeStruct((count // 2, 2 * GROUP, HD), jnp.bfloat16),
        ),
        in_specs=[
            pl.BlockSpec(memory_space=pltpu.SMEM),
            pl.BlockSpec(memory_space=pltpu.VMEM),
        ],
        out_specs=(
            pl.BlockSpec(memory_space=pltpu.VMEM),
            pl.BlockSpec(memory_space=pltpu.VMEM),
        ),
        scratch_shapes=[pltpu.VMEM((count * GROUP, HD), jnp.float32)],
        compiler_params=pltpu.CompilerParams(vmem_limit_bytes=8 << 20),
        name="dispatch",
    )(slot, q_rows)


def suffix_kernel(length_ref, q_ref, kv_ref, sum_ref, top_ref, total_ref):
    pairs = q_ref.shape[0]
    span = kv_ref.shape[2]
    lane = lax.broadcasted_iota(jnp.int32, (2 * GROUP, 2 * span), 1)
    second = lax.broadcasted_iota(jnp.int32, (2 * GROUP, 2 * span), 0) >= GROUP
    first_lane = jnp.where(second, span, 0)

    def one_pair(p):
        keys = kv_ref[pl.ds(2 * p, 2), 0].reshape(2 * span, HD)
        values = kv_ref[pl.ds(2 * p, 2), 1].reshape(2 * span, HD)
        scores = (
            lax.dot_general(q_ref[p], keys, NT, preferred_element_type=jnp.float32)
            * SCORE_SCALE
        )
        end_lane = first_lane + jnp.where(second, length_ref[2 * p + 1], length_ref[2 * p])
        live = (lane >= first_lane) & (lane < end_lane)
        top = jnp.max(jnp.where(live, scores, -jnp.inf), axis=-1, keepdims=True)
        weights = jnp.where(live, jnp.exp2(scores - top), 0.0)
        total = jnp.sum(weights, axis=-1, keepdims=True)
        weighted = jnp.dot(
            weights.astype(jnp.bfloat16), values, preferred_element_type=jnp.float32
        )
        shape = (2, GROUP, HD)
        sum_ref[pl.ds(2 * p, 2)] = weighted.reshape(shape)
        top_ref[pl.ds(2 * p, 2)] = jnp.broadcast_to(top, (2 * GROUP, HD)).reshape(shape)
        total_ref[pl.ds(2 * p, 2)] = jnp.broadcast_to(total, (2 * GROUP, HD)).reshape(shape)

    step = 8

    def body(s, carry):
        for u in range(step):
            one_pair(s * step + u)
        return carry

    lax.fori_loop(0, pairs // step, body, 0)


def suffix_attend(lengths, q_home, kv):
    count = lengths.shape[0]
    span = kv.shape[2]
    out = jax.ShapeDtypeStruct((count, GROUP, HD), jnp.float32)
    vmem = pl.BlockSpec(memory_space=pltpu.VMEM)
    return pl.pallas_call(
        suffix_kernel,
        out_shape=(out, out, out),
        in_specs=[pl.BlockSpec(memory_space=pltpu.SMEM), vmem, vmem],
        out_specs=(vmem, vmem, vmem),
        cost_estimate=pl.CostEstimate(
            flops=4 * count * GROUP * span * HD,
            bytes_accessed=kv.size * 2,
            transcendentals=count * GROUP * span,
        ),
        compiler_params=pltpu.CompilerParams(vmem_limit_bytes=12 << 20),
        name="suffix_attend",
    )(lengths, q_home, kv)


def prefix_kernel(q_ref, k_ref, v_ref, main_ref, stat_ref, s0_ref, s1_ref, m0_ref, m1_ref):
    rows = q_ref.shape[0]
    span = k_ref.shape[0]
    blocks = rows // BLOCK
    chunks = span // CHUNK
    per_home = SLOTS * GROUP
    homes = BLOCK // per_home

    def stage(ahead, s_ahead, m_ahead, now, s_now, m_now):
        if ahead is not None:
            q = q_ref[pl.ds(pl.multiple_of(ahead * BLOCK, BLOCK), BLOCK), :]
            top = jnp.full((BLOCK, HD), -jnp.inf, jnp.float32)
        if now is not None:
            shift = m_now[...]
            total = jnp.zeros((BLOCK, HD), jnp.float32)
            weighted = jnp.zeros((BLOCK, HD), jnp.float32)
        for c in range(chunks):
            at = c * CHUNK
            if ahead is not None:
                scores = lax.dot_general(
                    q, k_ref[at : at + CHUNK, :], NT, preferred_element_type=jnp.float32
                )
                s_ahead[:, at : at + CHUNK] = scores
                for l in range(0, CHUNK, HD):
                    top = jnp.maximum(top, scores[:, l : l + HD])
            if now is not None:
                parts = []
                for l in range(at, at + CHUNK, HD):
                    w = jnp.exp2(s_now[:, l : l + HD] * SCORE_SCALE - shift)
                    total = total + w
                    parts.append(w.astype(jnp.bfloat16))
                weighted = weighted + jnp.dot(
                    jnp.concatenate(parts, axis=1),
                    v_ref[at : at + CHUNK, :],
                    preferred_element_type=jnp.float32,
                )
        if ahead is not None:
            m_ahead[...] = jnp.broadcast_to(
                jnp.max(top, axis=-1, keepdims=True) * SCORE_SCALE, (BLOCK, HD)
            )
        if now is not None:
            mass = jnp.sum(total, axis=-1, keepdims=True)
            part = weighted / mass
            largest = jnp.max(jnp.abs(part), axis=-1, keepdims=True)
            step = jnp.ceil(jnp.log2(jnp.maximum(largest, 1e-30)) * 8.0)
            code = jnp.round(part * (jnp.exp2(step * -0.125) * CODE_TOP))
            code = jnp.clip(code, -CODE_TOP, CODE_TOP)
            start = pl.multiple_of(now * BLOCK, BLOCK)
            main_ref[pl.ds(start, BLOCK), :] = code.astype(jnp.int32).astype(jnp.int16)
            lse = shift[:, :1] + jnp.log2(mass)
            coarse = jnp.round(lse * 4.0)
            fine = jnp.round((lse - coarse * 0.25) * 131072.0)
            lane = lax.broadcasted_iota(jnp.int32, (BLOCK, HD), 1)
            inner = lax.broadcasted_iota(jnp.int32, (BLOCK, HD), 0) % per_home
            upper = jnp.where(lane == inner, coarse, 0.0) + jnp.where(
                lane == inner + per_home, step, 0.0
            )
            lower = jnp.where(lane == inner, fine, 0.0)
            upper = jnp.sum(upper.reshape(homes, per_home, HD), axis=1)
            lower = jnp.sum(lower.reshape(homes, per_home, HD), axis=1)
            first = pl.multiple_of(now * homes, homes)
            stat_ref[0, pl.ds(first, homes), :] = upper
            stat_ref[1, pl.ds(first, homes), :] = lower

    stage(0, s0_ref, m0_ref, None, None, None)

    def body(i, carry):
        stage(2 * i + 1, s1_ref, m1_ref, 2 * i, s0_ref, m0_ref)
        stage(2 * i + 2, s0_ref, m0_ref, 2 * i + 1, s1_ref, m1_ref)
        return carry

    lax.fori_loop(0, blocks // 2 - 1, body, 0)
    stage(blocks - 1, s1_ref, m1_ref, blocks - 2, s0_ref, m0_ref)
    stage(None, None, None, blocks - 1, s1_ref, m1_ref)


def prefix_attend(q_slots, prefix_kv):
    rows = q_slots.shape[0]
    span = prefix_kv.shape[3]
    homes = rows // (SLOTS * GROUP)
    whole = lambda *shape: pl.BlockSpec(shape, lambda i: (0,) * len(shape))
    return pl.pallas_call(
        prefix_kernel,
        grid=(1,),
        out_shape=(
            jax.ShapeDtypeStruct((rows, HD), jnp.int16),
            jax.ShapeDtypeStruct((2, homes, HD), jnp.float32),
        ),
        in_specs=[
            whole(rows, HD),
            pl.BlockSpec((None, None, None, span, HD), lambda i: (0, 0, 0, 0, 0)),
            pl.BlockSpec((None, None, None, span, HD), lambda i: (0, 1, 0, 0, 0)),
        ],
        out_specs=(whole(rows, HD), whole(2, homes, HD)),
        scratch_shapes=[
            pltpu.VMEM((BLOCK, span), jnp.float32),
            pltpu.VMEM((BLOCK, span), jnp.float32),
            pltpu.VMEM((BLOCK, HD), jnp.float32),
            pltpu.VMEM((BLOCK, HD), jnp.float32),
        ],
        cost_estimate=pl.CostEstimate(
            flops=4 * rows * span * HD,
            bytes_accessed=prefix_kv.size * 2,
            transcendentals=rows * span,
        ),
        compiler_params=pltpu.CompilerParams(vmem_limit_bytes=24 << 20),
        name="prefix_attend",
    )(q_slots, prefix_kv, prefix_kv)


def combine_kernel(slot_ref, main_ref, stat_ref, sum_ref, top_ref, total_ref, out_ref, tile_ref):
    tensor, rows, width = out_ref.shape
    lane = lax.broadcasted_iota(jnp.int32, (GROUP, HD), 1)
    head = lax.broadcasted_iota(jnp.int32, (GROUP, HD), 0)
    for t in range(tensor):
        for i in range(rows):
            r = t * rows + i
            slot = slot_ref[r]
            stats = jnp.broadcast_to(stat_ref[pl.ds(slot // SLOTS, 1), :], (GROUP, HD))
            at = head + (slot % SLOTS) * GROUP
            lse = jnp.sum(jnp.where(lane == at, stats, 0.0), axis=-1, keepdims=True)
            scale = jnp.sum(
                jnp.where(lane == at + SLOTS * GROUP, stats, 0.0), axis=-1, keepdims=True
            )
            part = main_ref[slot].astype(jnp.int32).astype(jnp.float32) * scale
            top = top_ref[r]
            joint = jnp.maximum(top, lse)
            prefix_mass = jnp.exp2(lse - joint)
            suffix_mass = jnp.exp2(top - joint)
            result = (prefix_mass * part + suffix_mass * sum_ref[r]) / (
                prefix_mass + suffix_mass * total_ref[r]
            )
            tile_ref[pl.ds(t * GROUP * rows + i, GROUP, stride=rows), :] = result
        for h in range(GROUP):
            out_ref[t, :, h * HD : (h + 1) * HD] = tile_ref[
                pl.ds((t * GROUP + h) * rows, rows), :
            ].astype(jnp.bfloat16)


def combine(slot, main, stats, suffix, tensor):
    count = slot.shape[0]
    vmem = pl.BlockSpec(memory_space=pltpu.VMEM)
    return pl.pallas_call(
        combine_kernel,
        out_shape=jax.ShapeDtypeStruct((tensor, count // tensor, GROUP * HD), jnp.bfloat16),
        in_specs=[pl.BlockSpec(memory_space=pltpu.SMEM)] + [vmem] * 5,
        out_specs=vmem,
        scratch_shapes=[pltpu.VMEM((count * GROUP, HD), jnp.float32)],
        compiler_params=pltpu.CompilerParams(vmem_limit_bytes=8 << 20),
        name="combine",
    )(slot, main, stats, *suffix)


def on_device(queries, suffix_kv, suffix_lengths, prefix_kv, tree_ids, owner_map):
    owners = lax.axis_size("prefix")
    tensor = lax.axis_size("tensor")
    rows = queries.shape[0]
    count = tree_ids.shape[0]
    width = GROUP * HD
    local_q = lax.all_to_all(queries, "tensor", split_axis=1, concat_axis=0, tiled=True)
    q_rows = local_q.reshape(tensor, rows, width)

    prompt = jnp.arange(owner_map.shape[0], dtype=jnp.int32)
    owner_row = jnp.sum(jnp.where(tree_ids[:, None] == prompt[None, :], owner_map[None, :], 0), axis=1)
    place = jnp.arange(count, dtype=jnp.int32)
    earlier = (tree_ids[:, None] == tree_ids[None, :]) & (place[None, :] < place[:, None])
    slot = owner_row * SLOTS + jnp.sum(earlier.astype(jnp.int32), axis=1)

    outgoing, q_home = dispatch(slot, q_rows)
    arrived = lax.all_to_all(
        outgoing.reshape(owners, SLOTS * GROUP, HD), "prefix", split_axis=0, concat_axis=0, tiled=True
    )
    suffix = suffix_attend(suffix_lengths, q_home, suffix_kv[:, :, 0])
    main, stats = prefix_attend(arrived.reshape(owners * SLOTS * GROUP, HD), prefix_kv)
    pairs = SLOTS * GROUP // 2
    stats = jnp.swapaxes(stats, 0, 1).astype(jnp.int16).reshape(owners, 1, 2, HD)
    sent = jnp.concatenate([main.reshape(owners, pairs, 2, HD), stats], axis=1)
    back = lax.all_to_all(sent, "prefix", split_axis=0, concat_axis=0, tiled=True)
    back_main = back[:, :pairs].reshape(owners * SLOTS, GROUP, HD)
    upper = back[:, pairs, 0].astype(jnp.float32)
    lower = back[:, pairs, 1].astype(jnp.float32)
    lane = lax.broadcasted_iota(jnp.int32, (owners, HD), 1)
    back_stats = jnp.where(
        lane < SLOTS * GROUP,
        upper * 0.25 + lower * (1.0 / 131072.0),
        jnp.exp2(upper * 0.125) * (1.0 / CODE_TOP),
    )
    attended = combine(slot, back_main, back_stats, suffix, tensor)
    done = lax.all_to_all(attended, "tensor", split_axis=0, concat_axis=0, tiled=True)
    return jnp.swapaxes(done, 0, 1).reshape(rows, tensor * width)


def solution(mesh):
    in_specs = (
        P(("prefix", "tensor"), None),
        P("prefix", None, "tensor", None, None),
        P("prefix"),
        P("prefix", None, "tensor", None, None),
        P("prefix"),
        P(),
    )
    out_specs = P(("prefix", "tensor"), None)
    return jax.shard_map(
        on_device, mesh=mesh, in_specs=in_specs, out_specs=out_specs, check_vma=False
    )
```

time: 150 us -> 102 us (0.68)
  waiting for transfers between devices: 59.3 us -> 15.8 us
  Pallas kernels: 0 us -> 18.2 us
  starting transfers between devices: 33.5 us -> 17.3 us
  blocking collectives: 34.8 us -> 45.9 us
  matrix products: 10.7 us -> 0 us
  local copies, waits for them, and re-layouts: 6.28 us -> 2.52 us
  other arithmetic: 4.47 us -> 1.93 us
    all_to_all x3 -> x1, waiting for transfers between devices: 55.1 us -> 11.4 us  [on_device(): lax.all_to_all(sent, 'prefix', split_axis=0, concat_axis=0, tiled=True)]
    pallas_call x0 -> x4, Pallas kernels: none -> 18.2 us  [the longest x1 8.44 us: suffix_attend(): pl.pallas_call(suffix_kernel, out_shape=(out, out, out), in_specs=[pl.Blo...]
    all_to_all x3 -> x1, starting transfers between devices: 23.4 us -> 7.18 us  [on_device(): lax.all_to_all(sent, 'prefix', split_axis=0, concat_axis=0, tiled=True)]
    all_to_all x2, blocking collectives: 34.8 us -> 45.9 us  [the longest x1 33.3 us: on_device(): lax.all_to_all(outgoing.reshape(owners, SLOTS * GROUP, HD), 'prefix', spl...]
    dot_general x10 -> x0, matrix products: 10.7 us -> none  [the longest x2 2.91 us: attend_piece(): jnp.einsum('skgin,gnd->skgid', weights.astype(jnp.bfloat16), value_rows,...]
    reduce_sum x4 -> x1, other arithmetic: 4.18 us -> 0.91 us  [on_device(): jnp.sum(jnp.where(tree_ids[:, None] == prompt[None, :], owner_map[None, :...]
    squeeze x1 -> x0, local copies, waits for them, and re-layouts: 1.68 us -> none  [on_device(): value_rows = prefix_kv[0, 1]]
    unnamed x5 -> x7, local copies, waits for them, and re-layouts: 0.73 us -> 2.25 us
  transfers between devices with their start and end apart: 4 -> 2, of which waited for: 4 -> 2; matrix products, arithmetic and copies ran while one was open for 5% -> 1% of each run, Pallas kernels for 0% -> 8%
where the time goes in v1:
time: 102 us
  blocking collectives  45.9 us (45%)
  Pallas kernels  18.2 us (18%)
  starting transfers between devices  17.3 us (17%)
  waiting for transfers between devices  15.8 us (15%)
  local copies, waits for them, and re-layouts  2.52 us (2%)
  other arithmetic  1.93 us (2%)
    all_to_all x1, blocking collectives, on_device(): lax.all_to_all(outgoing.reshape(owners, SLOTS * GROUP, HD), 'prefix', spl...  33.3 us
    all_to_all x1, blocking collectives, on_device(): lax.all_to_all(attended, 'tensor', split_axis=0, concat_axis=0, tiled=True)  12.6 us
    all_to_all x1, waiting for transfers between devices, on_device(): lax.all_to_all(sent, 'prefix', split_axis=0, concat_axis=0, tiled=True)  11.4 us
    all_to_all x1, starting transfers between devices, on_device(): lax.all_to_all(queries, 'tensor', split_axis=1, concat_axis=0, tiled=True)  10.1 us
    pallas_call x1, Pallas kernels, suffix_attend(): pl.pallas_call(suffix_kernel, out_shape=(out, out, out), in_specs=[pl.Blo...  8.44 us
    pallas_call x1, Pallas kernels, prefix_attend(): pl.pallas_call(prefix_kernel, grid=(1,), out_shape=(jax.ShapeDtypeStruct(...  8.03 us
    all_to_all x1, starting transfers between devices, on_device(): lax.all_to_all(sent, 'prefix', split_axis=0, concat_axis=0, tiled=True)  7.18 us
    all_to_all x1, waiting for transfers between devices, on_device(): lax.all_to_all(queries, 'tensor', split_axis=1, concat_axis=0, tiled=True)  4.35 us
  transfers between devices with their start and end apart: 2, of which 2 were waited for; matrix products, arithmetic and copies ran while one was open for 1% of the time, Pallas kernels for 8%

profile of v1, /device:TPU:1, one launch (start us, length us, event | category | flops | bytes accessed | tf_op | source)
XLA Modules:
  0.0 101.7 jit_solution(7268480060665581209)
XLA Ops:
  0.0 10.1 %all-to-all-start = ((bf16[8,8,1024]{2,0,1:T(8,128)(2,1)}), bf16[8,8,1024]{2,0,1:T(8,128)(2,1)S(1)}, u32[]{:S(2)}, u32[]{:S(2)}) async-start(bf16[8,8,1024]{2,0,1:T(8,128)(2,1)} %bitcast.29), calls=%async_computation | async-start | bytes 262144 | tf_op jit(solution)/shard_map/all_to_all | solution.py:281
  10.1 0.9 select_reduce_fusion
  11.0 4.3 %all-to-all-done = bf16[8,8,1024]{2,0,1:T(8,128)(2,1)S(1)} async-done(((bf16[8,8,1024]{2,0,1:T(8,128)(2,1)}), bf16[8,8,1024]{2,0,1:T(8,128)(2,1)S(1)}, u32[]{:S(2)}, u32[]{:S(2)}) %all-to-all-start) | async-done | bytes 131104 | tf_op jit(solution)/shard_map/all_to_all | solution.py:281
  15.4 0.6 dispatch.1
  16.0 33.3 %all_to_all.31 = bf16[64,16,128]{2,1,0:T(8,128)(2,1)S(1)} all-to-all(bf16[64,16,128]{2,1,0:T(8,128)(2,1)S(1)} %bitcast.26), channel_id=1, replica_groups=mesh['prefix'=64,'tensor'=8] {'prefix'}, dimensions={0} | all-to-all | bytes 524288 | tf_op jit(solution)/shard_map/all_to_all | solution.py:291
  49.3 0.0 copy-start.2
  49.3 1.6 %copy-done.2 = bf16[1,2,1,4096,128]{4,3,2,1,0:T(8,128)(2,1)S(1)} copy-done((bf16[1,2,1,4096,128]{4,3,2,1,0:T(8,128)(2,1)S(1)}, bf16[1,2,1,4096,128]{4,3,2,1,0:T(8,128)(2,1)}, u32[]{:S(2)}) %copy-start.2) | copy-done | bytes 2097176
  50.9 0.0 copy-start
  50.9 0.0 copy-start.1
  50.9 8.0 %prefix_attend.1 = (s16[1024,128]{1,0:T(8,128)(2,1)S(1)}, f32[2,64,128]{2,1,0:T(8,128)S(1)}) custom-call(bf16[1024,128]{1,0:T(8,128)(2,1)S(1)} %bitcast.27, bf16[1,2,1,4096,128]{4,3,2,1,0:T(8,128)(2,1)S(1)} %copy-done.2, bf16[1,2,1,4096,128]{4,3,2,1,0:T(8,128)(2,1)S(1)} %copy-done.2), custom_call_target="tpu_custom_call" | custom-call | flops 2147483648 | bytes 2097152 | tf_op jit(solution)/shard_map/prefix_attend/pallas_call | solution.py:203
  59.0 1.0 pad_add_fusion
  60.0 7.2 %all-to-all-start.2 = ((s16[64,9,2,128]{3,2,1,0:T(2,128)(2,1)}), s16[64,9,2,128]{3,2,1,0:T(2,128)(2,1)S(1)}, u32[]{:S(2)}, u32[]{:S(2)}) async-start(s16[64,9,2,128]{3,2,1,0:T(2,128)(2,1)} %pad_add_fusion), calls=%async_computation.2 | async-start | bytes 589824 | tf_op jit(solution)/shard_map/all_to_all | solution.py:299
  67.2 0.0 copy-done
  67.2 0.0 copy-done.1
  67.2 8.4 %suffix_attend.1 = (f32[64,8,128]{2,1,0:T(8,128)S(1)}, f32[64,8,128]{2,1,0:T(8,128)S(1)}, f32[64,8,128]{2,1,0:T(8,128)S(1)}) custom-call(s32[64]{0:T(128)S(1)} %copy-done.1, bf16[32,16,128]{2,1,0:T(8,128)(2,1)S(1)} %get-tuple-element.15.q_ref, bf16[64,2,64,128]{3,2,1,0:T(8,128)(2,1)S(1)} %bitcast.22), custom_call_target="tpu_custom_call" | custom-call | flops 16777216 | bytes 2097152 | tf_op jit(solution)/shard_map/suffix_attend/pallas_call | solution.py:107
  75.6 11.4 %all-to-all-done.2 = s16[64,9,2,128]{3,2,1,0:T(2,128)(2,1)S(1)} async-done(((s16[64,9,2,128]{3,2,1,0:T(2,128)(2,1)}), s16[64,9,2,128]{3,2,1,0:T(2,128)(2,1)S(1)}, u32[]{:S(2)}, u32[]{:S(2)}) %all-to-all-start.2) | async-done | bytes 294944 | tf_op jit(solution)/shard_map/all_to_all | solution.py:299
  87.2 0.2 slice.12
  87.3 1.1 %combine.1 = bf16[8,8,1024]{2,1,0:T(8,128)(2,1)S(1)} custom-call(s32[64]{0:T(128)S(1)} %multiply_add_fusion.slot_ref, s16[128,8,128]{2,1,0:T(8,128)(2,1)S(1)} %bitcast.23, f32[64,128]{1,0:T(8,128)S(1)} %fusion.2.stat_ref, f32[64,8,128]{2,1,0:T(8,128)S(1)} %get-tuple-element.16.sum_ref, f32[64,8,128]{2,1,0:T(8,128)S(1)} %get-tuple-element.17.top_ref, ...), custom_call_target="tpu_custom_call" | custom-call | tf_op jit(solution)/shard_map/combine/pallas_call | solution.py:264
  88.4 12.6 %all_to_all.32 = bf16[8,8,1024]{2,1,0:T(8,128)(2,1)S(1)} all-to-all(bf16[8,8,1024]{2,1,0:T(8,128)(2,1)S(1)} %combine.1), channel_id=1, replica_groups=mesh['prefix'=64,'tensor'=8] {'tensor'}, dimensions={0} | all-to-all | bytes 262144 | tf_op jit(solution)/shard_map/all_to_all | solution.py:310
  101.0 0.7 copy.20
  (6 shorter events, 0.1 us)
Async XLA Ops:
  0.0 15.4 %all-to-all-start = ((bf16[8,8,1024]{2,0,1:T(8,128)(2,1)}), bf16[8,8,1024]{2,0,1:T(8,128)(2,1)S(1)}, u32[]{:S(2)}, u32[]{:S(2)}) async-start(bf16[8,8,1024]{2,0,1:T(8,128)(2,1)} %bitcast.29), calls=%async_computation | async-start | bytes 262144 | tf_op jit(solution)/shard_map/all_to_all | solution.py:281
  49.3 1.6 %copy-start.2 = (bf16[1,2,1,4096,128]{4,3,2,1,0:T(8,128)(2,1)S(1)}, bf16[1,2,1,4096,128]{4,3,2,1,0:T(8,128)(2,1)}, u32[]{:S(2)}) copy-start(bf16[1,2,1,4096,128]{4,3,2,1,0:T(8,128)(2,1)} %v_ref.1) | copy-start | bytes 6291460
  50.9 16.3 %copy-start = (bf16[64,2,1,64,128]{4,3,2,1,0:T(8,128)(2,1)S(1)}, bf16[64,2,1,64,128]{4,3,2,1,0:T(8,128)(2,1)}, u32[]{:S(2)}) copy-start(bf16[64,2,1,64,128]{4,3,2,1,0:T(8,128)(2,1)} %param.7) | copy-start | bytes 6291460
  50.9 16.3 %copy-start.1 = (s32[64]{0:T(128)S(1)}, s32[64]{0:T(128)}, u32[]{:S(2)}) copy-start(s32[64]{0:T(128)} %length_ref.1) | copy-start | bytes 772
  60.0 27.1 %all-to-all-start.2 = ((s16[64,9,2,128]{3,2,1,0:T(2,128)(2,1)}), s16[64,9,2,128]{3,2,1,0:T(2,128)(2,1)S(1)}, u32[]{:S(2)}, u32[]{:S(2)}) async-start(s16[64,9,2,128]{3,2,1,0:T(2,128)(2,1)} %pad_add_fusion), calls=%async_computation.2 | async-start | bytes 589824 | tf_op jit(solution)/shard_map/all_to_all | solution.py:299

commit v2 on v1

v2 whole, which is shorter than its diff:
```python
import math

import jax
import jax.numpy as jnp
from jax import lax
from jax.experimental import pallas as pl
from jax.experimental.pallas import tpu as pltpu
from jax.sharding import PartitionSpec as P

H = 64
KVH = 8
HD = 128
GROUP = H // KVH
SLOTS = 2
CODE_TOP = 32767.0
SCORE_SCALE = math.log2(math.e) / math.sqrt(HD)

BLOCK = 256
CHUNK = 256
PAIRS = 8
PAIR = SLOTS * GROUP
SENT = PAIR + 2

NT = (((1,), (1,)), ((), ()))


def dispatch_kernel(slot_ref, q_ref, out_ref, home_ref, tile_ref):
    tensor, rows, width = q_ref.shape
    for t in range(tensor):
        for h in range(GROUP):
            tile_ref[pl.ds((t * GROUP + h) * rows, rows), :] = q_ref[
                t, :, h * HD : (h + 1) * HD
            ].astype(jnp.float32)
    for r in range(0, tensor * rows, 2):
        pair = []
        for k in range(2):
            t, i = divmod(r + k, rows)
            tile = tile_ref[pl.ds(t * GROUP * rows + i, GROUP, stride=rows), :]
            pair.append(tile)
            out_ref[slot_ref[r + k]] = tile.astype(jnp.bfloat16)
        home_ref[r // 2] = jnp.concatenate(pair, axis=0).astype(jnp.bfloat16)


def dispatch(slot, q_rows):
    tensor, rows, width = q_rows.shape
    count = tensor * rows
    owners = count
    return pl.pallas_call(
        dispatch_kernel,
        out_shape=(
            jax.ShapeDtypeStruct((owners * SLOTS, GROUP, HD), jnp.bfloat16),
            jax.ShapeDtypeStruct((count // 2, 2 * GROUP, HD), jnp.bfloat16),
        ),
        in_specs=[
            pl.BlockSpec(memory_space=pltpu.SMEM),
            pl.BlockSpec(memory_space=pltpu.VMEM),
        ],
        out_specs=(
            pl.BlockSpec(memory_space=pltpu.VMEM),
            pl.BlockSpec(memory_space=pltpu.VMEM),
        ),
        scratch_shapes=[pltpu.VMEM((count * GROUP, HD), jnp.float32)],
        compiler_params=pltpu.CompilerParams(vmem_limit_bytes=8 << 20),
        name="dispatch",
    )(slot, q_rows)


def suffix_kernel(length_ref, q_ref, kv_ref, prefix_ref, part_ref, lse_ref, keys_ref, turned_ref):
    pairs = q_ref.shape[0]
    span = kv_ref.shape[2]
    lane = lax.broadcasted_iota(jnp.int32, (2 * GROUP, 2 * span), 1)
    second = lax.broadcasted_iota(jnp.int32, (2 * GROUP, 2 * span), 0) >= GROUP
    first_lane = jnp.where(second, span, 0)

    def some_pairs(first):
        scores, live = [], []
        for u in range(PAIRS):
            p = first + u
            keys = kv_ref[pl.ds(2 * p, 2), 0].reshape(2 * span, HD)
            scores.append(
                lax.dot_general(q_ref[p], keys, NT, preferred_element_type=jnp.float32)
            )
            end_lane = first_lane + jnp.where(second, length_ref[2 * p + 1], length_ref[2 * p])
            live.append((lane >= first_lane) & (lane < end_lane))
        masked = [
            jnp.where(m, x * SCORE_SCALE, -jnp.inf) for m, x in zip(live, scores)
        ]
        tops = [jnp.max(x, axis=-1, keepdims=True) for x in masked]
        weights = [jnp.exp2(x - t) for x, t in zip(masked, tops)]
        totals = [jnp.sum(w, axis=-1, keepdims=True) for w in weights]
        sums = []
        for u in range(PAIRS):
            values = kv_ref[pl.ds(2 * (first + u), 2), 1].reshape(2 * span, HD)
            sums.append(
                jnp.dot(
                    weights[u].astype(jnp.bfloat16), values, preferred_element_type=jnp.float32
                )
            )
        shape = (2, GROUP, HD)
        for u in range(PAIRS):
            at = pl.ds(2 * (first + u), 2)
            part_ref[at] = (sums[u] / totals[u]).reshape(shape)
            lse = tops[u] + jnp.log2(totals[u])
            lse_ref[at] = jnp.broadcast_to(lse, (2 * GROUP, HD)).reshape(shape)

    def body(s, carry):
        some_pairs(s * PAIRS)
        return carry

    lax.fori_loop(0, pairs // PAIRS, body, 0)
    keys_ref[...] = prefix_ref[0, 0, 0]
    for at in range(0, prefix_ref.shape[3], 2 * HD):
        turned_ref[:, at : at + 2 * HD] = prefix_ref[0, 1, 0, at : at + 2 * HD, :].T


def suffix_attend(lengths, q_home, kv, prefix_kv):
    count = lengths.shape[0]
    span = kv.shape[2]
    out = jax.ShapeDtypeStruct((count, GROUP, HD), jnp.float32)
    vmem = pl.BlockSpec(memory_space=pltpu.VMEM)
    return pl.pallas_call(
        suffix_kernel,
        out_shape=(out, out, jax.ShapeDtypeStruct((prefix_kv.shape[3], HD), jnp.bfloat16), jax.ShapeDtypeStruct((HD, prefix_kv.shape[3]), jnp.bfloat16)),
        in_specs=[pl.BlockSpec(memory_space=pltpu.SMEM), vmem, vmem, vmem],
        out_specs=(vmem, vmem, vmem, vmem),
        cost_estimate=pl.CostEstimate(
            flops=4 * count * GROUP * span * HD,
            bytes_accessed=(kv.size + prefix_kv.size) * 2,
            transcendentals=count * GROUP * span,
        ),
        compiler_params=pltpu.CompilerParams(vmem_limit_bytes=16 << 20),
        name="suffix_attend",
    )(lengths, q_home, kv, prefix_kv)


def prefix_kernel(
    q_ref, k_ref, vt_ref, sent_ref, s0_ref, s1_ref, m0_ref, m1_ref
):
    rows = q_ref.shape[0]
    span = k_ref.shape[0]
    blocks = rows // BLOCK
    chunks = span // CHUNK
    homes = HD // PAIR

    def fold(x, op):
        return op(x.reshape(CHUNK // 8, 8, BLOCK), axis=0)

    def finish(now, weighted, mass, shift):
        part = weighted / mass
        largest = jnp.max(jnp.abs(part), axis=0, keepdims=True)
        step = jnp.ceil(jnp.log2(jnp.maximum(largest, 1e-30)) * 8.0)
        code = jnp.round(part * (jnp.exp2(step * -0.125) * CODE_TOP))
        code = jnp.clip(code, -CODE_TOP, CODE_TOP)
        lse = shift + jnp.log2(mass)
        coarse = jnp.round(lse * 4.0)
        fine = jnp.round((lse - coarse * 0.25) * 131072.0)
        lane = lax.broadcasted_iota(jnp.int32, (homes, HD), 1)
        home = lax.broadcasted_iota(jnp.int32, (homes, HD), 0)
        mine = lane // PAIR == home
        other = ((lane + HD // 2) % HD) // PAIR == home
        for g in range(BLOCK // HD):
            cut = slice(g * HD, (g + 1) * HD)
            rows_code = code[:, cut].T
            wide = lambda x: jnp.broadcast_to(x, (homes, HD))
            upper = jnp.where(mine, wide(coarse[:, cut]), 0.0)
            turned = pltpu.roll(wide(step[:, cut]), HD // 2, 1)
            upper = upper + jnp.where(other, turned, 0.0)
            lower = jnp.where(mine, wide(fine[:, cut]), 0.0)
            pieces = []
            for u in range(homes):
                pieces += [
                    rows_code[u * PAIR : (u + 1) * PAIR],
                    upper[u : u + 1],
                    lower[u : u + 1],
                ]
            packed = jnp.concatenate(pieces, axis=0).astype(jnp.int32).astype(jnp.int16)
            size = homes * SENT
            start = pl.multiple_of((now * (BLOCK // HD) + g) * size, size)
            sent_ref[pl.ds(start, size), :] = packed

    def stage(ahead, s_ahead, m_ahead, now, s_now, m_now):
        if ahead is not None:
            q = q_ref[pl.ds(pl.multiple_of(ahead * BLOCK, BLOCK), BLOCK), :]
            top = jnp.full((8, BLOCK), -jnp.inf, jnp.float32)
        if now is not None:
            shift = m_now[0:1, :]
            total = jnp.zeros((8, BLOCK), jnp.float32)
            weighted = jnp.zeros((HD, BLOCK), jnp.float32)
        for c in range(chunks):
            at = c * CHUNK
            if ahead is not None:
                scores = lax.dot_general(
                    k_ref[at : at + CHUNK, :], q, NT, preferred_element_type=jnp.float32
                )
                s_ahead[at : at + CHUNK, :] = scores
                top = jnp.maximum(top, fold(scores, jnp.max))
            if now is not None:
                w = jnp.exp2(s_now[at : at + CHUNK, :] * SCORE_SCALE - shift)
                total = total + fold(w, jnp.sum)
                weighted = weighted + jnp.dot(
                    vt_ref[:, at : at + CHUNK],
                    w.astype(jnp.bfloat16),
                    preferred_element_type=jnp.float32,
                )
        if ahead is not None:
            m_ahead[...] = jnp.broadcast_to(
                jnp.max(top, axis=0, keepdims=True) * SCORE_SCALE, (8, BLOCK)
            )
        if now is not None:
            finish(now, weighted, jnp.sum(total, axis=0, keepdims=True), shift)

    stage(0, s0_ref, m0_ref, None, None, None)
    for b in range(blocks - 1):
        even, odd = (s0_ref, m0_ref), (s1_ref, m1_ref)
        if b % 2 == 0:
            stage(b + 1, *odd, b, *even)
        else:
            stage(b + 1, *even, b, *odd)
    stage(None, None, None, blocks - 1, s1_ref, m1_ref)


def prefix_attend(q_slots, keys, values_t):
    rows = q_slots.shape[0]
    span = keys.shape[0]
    homes = rows // PAIR
    vmem = pl.BlockSpec(memory_space=pltpu.VMEM)
    return pl.pallas_call(
        prefix_kernel,
        out_shape=jax.ShapeDtypeStruct((homes * SENT, HD), jnp.int16),
        in_specs=[vmem] * 3,
        out_specs=vmem,
        scratch_shapes=[
            pltpu.VMEM((span, BLOCK), jnp.float32),
            pltpu.VMEM((span, BLOCK), jnp.float32),
            pltpu.VMEM((8, BLOCK), jnp.float32),
            pltpu.VMEM((8, BLOCK), jnp.float32),
        ],
        cost_estimate=pl.CostEstimate(
            flops=4 * rows * span * HD,
            bytes_accessed=keys.size * 4,
            transcendentals=rows * span,
        ),
        compiler_params=pltpu.CompilerParams(vmem_limit_bytes=24 << 20),
        name="prefix_attend",
    )(q_slots, keys, values_t)


def combine_kernel(
    slot_ref, back_ref, part_ref, lse_ref, out_ref, back32_ref, tile_ref
):
    tensor, rows, width = out_ref.shape
    lane = lax.broadcasted_iota(jnp.int32, (GROUP, HD), 1)
    head = lax.broadcasted_iota(jnp.int32, (GROUP, HD), 0)
    own = (slot_ref[tensor * rows] % (HD // PAIR)) * PAIR
    own_step = (own + HD // 2) % HD
    for k in range(0, back_ref.shape[0], 16):
        back32_ref[k : k + 16, :] = back_ref[k : k + 16, :].astype(jnp.int32).astype(jnp.float32)
    for t in range(tensor):
        for i in range(rows):
            r = t * rows + i
            slot = slot_ref[r]
            base = (slot // SLOTS) * SENT
            inner = (slot % SLOTS) * GROUP
            upper = back32_ref[pl.ds(base + PAIR, 1), :]
            lower = back32_ref[pl.ds(base + PAIR + 1, 1), :]
            at = head + inner

            def pick(row, where):
                wide = jnp.broadcast_to(row, (GROUP, HD))
                return jnp.sum(jnp.where(lane == where, wide, 0.0), axis=-1, keepdims=True)

            lse = pick(upper * 0.25 + lower * (1.0 / 131072.0), at + own)
            step = pick(upper, at + own_step)
            scale = jnp.exp2(step * 0.125) * (1.0 / CODE_TOP)
            part = back32_ref[pl.ds(base + inner, GROUP), :] * scale
            suffix_lse = lse_ref[r]
            joint = jnp.maximum(suffix_lse, lse)
            prefix_mass = jnp.exp2(lse - joint)
            suffix_mass = jnp.exp2(suffix_lse - joint)
            result = (prefix_mass * part + suffix_mass * part_ref[r]) / (
                prefix_mass + suffix_mass
            )
            tile_ref[pl.ds(t * GROUP * rows + i, GROUP, stride=rows), :] = result
        for h in range(GROUP):
            out_ref[t, :, h * HD : (h + 1) * HD] = tile_ref[
                pl.ds((t * GROUP + h) * rows, rows), :
            ].astype(jnp.bfloat16)


def combine(slot, back, suffix, tensor):
    count = slot.shape[0] - 1
    vmem = pl.BlockSpec(memory_space=pltpu.VMEM)
    smem = pl.BlockSpec(memory_space=pltpu.SMEM)
    return pl.pallas_call(
        combine_kernel,
        out_shape=jax.ShapeDtypeStruct((tensor, count // tensor, GROUP * HD), jnp.bfloat16),
        in_specs=[smem] + [vmem] * 3,
        out_specs=vmem,
        scratch_shapes=[
            pltpu.VMEM(back.shape, jnp.float32),
            pltpu.VMEM((count * GROUP, HD), jnp.float32),
        ],
        compiler_params=pltpu.CompilerParams(vmem_limit_bytes=8 << 20),
        name="combine",
    )(slot, back, *suffix)


def on_device(queries, suffix_kv, suffix_lengths, prefix_kv, tree_ids, owner_map):
    owners = lax.axis_size("prefix")
    tensor = lax.axis_size("tensor")
    rows = queries.shape[0]
    count = tree_ids.shape[0]
    width = GROUP * HD
    local_q = lax.all_to_all(queries, "tensor", split_axis=1, concat_axis=0, tiled=True)
    q_rows = local_q.reshape(tensor, rows, width)

    prompt = jnp.arange(owner_map.shape[0], dtype=jnp.int32)
    owner_row = jnp.sum(jnp.where(tree_ids[:, None] == prompt[None, :], owner_map[None, :], 0), axis=1)
    place = jnp.arange(count, dtype=jnp.int32)
    earlier = (tree_ids[:, None] == tree_ids[None, :]) & (place[None, :] < place[:, None])
    slot = owner_row * SLOTS + jnp.sum(earlier.astype(jnp.int32), axis=1)

    home = lax.axis_index("prefix").astype(jnp.int32)
    slot = jnp.concatenate([slot, home.reshape(1)])
    outgoing, q_home = dispatch(slot, q_rows)
    arrived = lax.all_to_all(
        outgoing.reshape(owners, SLOTS * GROUP, HD), "prefix", split_axis=0, concat_axis=0, tiled=True
    )
    *suffix, keys, values_t = suffix_attend(suffix_lengths, q_home, suffix_kv[:, :, 0], prefix_kv)
    packed = prefix_attend(arrived.reshape(owners * PAIR, HD), keys, values_t)
    back = lax.all_to_all(
        packed.reshape(owners, SENT // 2, 2, HD), "prefix", split_axis=0, concat_axis=0, tiled=True
    )
    attended = combine(slot, back.reshape(owners * SENT, HD), suffix, tensor)
    done = lax.all_to_all(attended, "tensor", split_axis=0, concat_axis=0, tiled=True)
    return jnp.swapaxes(done, 0, 1).reshape(rows, tensor * width)


def solution(mesh):
    in_specs = (
        P(("prefix", "tensor"), None),
        P("prefix", None, "tensor", None, None),
        P("prefix"),
        P("prefix", None, "tensor", None, None),
        P("prefix"),
        P(),
    )
    out_specs = P(("prefix", "tensor"), None)
    return jax.shard_map(
        on_device, mesh=mesh, in_specs=in_specs, out_specs=out_specs, check_vma=False
    )
```

time: 102 us -> 97.9 us (0.960)
  Pallas kernels: 18.2 us -> 11.1 us
  starting transfers between devices: 17.3 us -> 24.2 us
  blocking collectives: 45.9 us -> 39.5 us
  local copies, waits for them, and re-layouts: 2.52 us -> 4.49 us
  waiting for transfers between devices: 15.8 us -> 17.2 us
    pallas_call x2, Pallas kernels: 16.5 us -> 8.64 us  [the longest x1 6.01 us: prefix_attend(): pl.pallas_call(prefix_kernel, out_shape=jax.ShapeDtypeStruct((homes * SEN...]
    all_to_all x1, starting transfers between devices: 7.18 us -> 14.1 us  [on_device(): lax.all_to_all(outgoing.reshape(owners, SLOTS * GROUP, HD), 'prefix', spl...]
    all_to_all x1, blocking collectives: 33.3 us -> 26.9 us  [on_device(): lax.all_to_all(packed.reshape(owners, SENT // 2, 2, HD), 'prefix', split_...]
    unnamed x7, local copies, waits for them, and re-layouts: 2.25 us -> 4.49 us
    all_to_all x1, waiting for transfers between devices: 11.4 us -> 12.9 us  [on_device(): lax.all_to_all(outgoing.reshape(owners, SLOTS * GROUP, HD), 'prefix', spl...]
  transfers between devices with their start and end apart: 2 -> 2, of which waited for: 2 -> 2; matrix products, arithmetic and copies ran while one was open for 1% -> 1% of each run, Pallas kernels for 8% -> 3%
where the time goes in v2:
time: 97.9 us; the launch traced here: 97.5 us
  blocking collectives  39.5 us (40%)
  starting transfers between devices  24.2 us (25%)
  waiting for transfers between devices  17.2 us (18%)
  Pallas kernels  11.1 us (11%)
  local copies, waits for them, and re-layouts  4.49 us (5%)
  other arithmetic  0.99 us (1%)
    all_to_all x1, blocking collectives, on_device(): lax.all_to_all(packed.reshape(owners, SENT // 2, 2, HD), 'prefix', split_...  26.9 us
    all_to_all x1, starting transfers between devices, on_device(): lax.all_to_all(outgoing.reshape(owners, SLOTS * GROUP, HD), 'prefix', spl...  14.1 us
    all_to_all x1, waiting for transfers between devices, on_device(): lax.all_to_all(outgoing.reshape(owners, SLOTS * GROUP, HD), 'prefix', spl...  12.9 us
    all_to_all x1, blocking collectives, on_device(): lax.all_to_all(attended, 'tensor', split_axis=0, concat_axis=0, tiled=True)  12.6 us
    all_to_all x1, starting transfers between devices, on_device(): lax.all_to_all(queries, 'tensor', split_axis=1, concat_axis=0, tiled=True)  10.1 us
    pallas_call x1, Pallas kernels, prefix_attend(): pl.pallas_call(prefix_kernel, out_shape=jax.ShapeDtypeStruct((homes * SEN...  6.01 us
    unnamed x7, local copies, waits for them, and re-layouts  4.49 us
    all_to_all x1, waiting for transfers between devices, on_device(): lax.all_to_all(queries, 'tensor', split_axis=1, concat_axis=0, tiled=True)  4.26 us
  transfers between devices with their start and end apart: 2, of which 2 were waited for; matrix products, arithmetic and copies ran while one was open for 1% of the time, Pallas kernels for 3%

profile of v2, /device:TPU:1, one launch (start us, length us, event | category | flops | bytes accessed | tf_op | source)
XLA Modules:
  0.0 97.5 jit_solution(15584771080705026219)
XLA Ops:
  0.0 10.1 %all-to-all-start = ((bf16[8,8,1024]{2,0,1:T(8,128)(2,1)}), bf16[8,8,1024]{2,0,1:T(8,128)(2,1)S(1)}, u32[]{:S(2)}, u32[]{:S(2)}) async-start(bf16[8,8,1024]{2,0,1:T(8,128)(2,1)} %bitcast.17), calls=%async_computation | async-start | bytes 262144 | tf_op jit(solution)/shard_map/all_to_all | solution.py:314
  10.1 0.9 select_reduce_fusion
  11.0 0.1 pad_add_fusion.slot_ref
  11.1 4.3 %all-to-all-done = bf16[8,8,1024]{2,0,1:T(8,128)(2,1)S(1)} async-done(((bf16[8,8,1024]{2,0,1:T(8,128)(2,1)}), bf16[8,8,1024]{2,0,1:T(8,128)(2,1)S(1)}, u32[]{:S(2)}, u32[]{:S(2)}) %all-to-all-start) | async-done | bytes 131104 | tf_op jit(solution)/shard_map/all_to_all | solution.py:314
  15.4 1.3 %dispatch.1 = (bf16[128,8,128]{2,1,0:T(8,128)(2,1)}, bf16[32,16,128]{2,1,0:T(8,128)(2,1)S(1)}) custom-call(s32[65]{0:T(128)S(1)} %pad_add_fusion.slot_ref, bf16[8,8,1024]{2,1,0:T(8,128)(2,1)S(1)} %bitcast.13), custom_call_target="tpu_custom_call" | custom-call | tf_op jit(solution)/shard_map/dispatch/pallas_call | solution.py:48
  16.7 14.1 %all-to-all-start.1 = ((bf16[64,16,128]{2,1,0:T(8,128)(2,1)}), bf16[64,16,128]{2,1,0:T(8,128)(2,1)S(1)}, u32[]{:S(2)}, u32[]{:S(2)}) async-start(bf16[64,16,128]{2,1,0:T(8,128)(2,1)} %bitcast.3), calls=%async_computation.1 | async-start | bytes 524288 | tf_op jit(solution)/shard_map/all_to_all | solution.py:326
  30.8 0.0 copy-start
  30.8 1.6 %copy-done = bf16[64,2,1,64,128]{4,3,2,1,0:T(8,128)(2,1)S(1)} copy-done((bf16[64,2,1,64,128]{4,3,2,1,0:T(8,128)(2,1)S(1)}, bf16[64,2,1,64,128]{4,3,2,1,0:T(8,128)(2,1)}, u32[]{:S(2)}) %copy-start) | copy-done | bytes 2097176
  32.4 0.0 copy-start.1
  32.4 1.6 %copy-done.1 = bf16[1,2,1,4096,128]{4,3,2,1,0:T(8,128)(2,1)S(1)} copy-done((bf16[1,2,1,4096,128]{4,3,2,1,0:T(8,128)(2,1)S(1)}, bf16[1,2,1,4096,128]{4,3,2,1,0:T(8,128)(2,1)}, u32[]{:S(2)}) %copy-start.1) | copy-done | bytes 2097176
  34.0 0.0 copy-start.2
  34.0 0.7 copy-done.2
  34.6 2.6 %suffix_attend.1 = (f32[64,8,128]{2,1,0:T(8,128)S(1)}, f32[64,8,128]{2,1,0:T(8,128)S(1)}, bf16[4096,128]{1,0:T(8,128)(2,1)S(1)}, bf16[128,4096]{1,0:T(8,128)(2,1)S(1)}) custom-call(s32[64]{0:T(128)S(1)} %copy-done.2, bf16[32,16,128]{2,1,0:T(8,128)(2,1)S(1)} %get-tuple-element.12.q_ref, bf16[64,2,64,128]{3,2,1,0:T(8,128)(2,1)S(1)} %bitcast.11, ...), custom_call_target="tpu_custom_call" | custom-call | flops 16777216 | bytes 4194304 | tf_op jit(solution)/shard_map/suffix_attend/pallas_call | solution.py:121
  37.3 12.9 %all-to-all-done.1 = bf16[64,16,128]{2,1,0:T(8,128)(2,1)S(1)} async-done(((bf16[64,16,128]{2,1,0:T(8,128)(2,1)}), bf16[64,16,128]{2,1,0:T(8,128)(2,1)S(1)}, u32[]{:S(2)}, u32[]{:S(2)}) %all-to-all-start.1) | async-done | bytes 262176 | tf_op jit(solution)/shard_map/all_to_all | solution.py:326
  50.2 6.0 %prefix_attend.1 = s16[1152,128]{1,0:T(8,128)(2,1)S(1)} custom-call(bf16[1024,128]{1,0:T(8,128)(2,1)S(1)} %bitcast.15, bf16[4096,128]{1,0:T(8,128)(2,1)S(1)} %get-tuple-element.13.k_ref, bf16[128,4096]{1,0:T(8,128)(2,1)S(1)} %get-tuple-element.14.vt_ref), custom_call_target="tpu_custom_call" | custom-call | flops 2147483648 | bytes 2097152 | tf_op jit(solution)/shard_map/prefix_attend/pallas_call | solution.py:227
  56.2 26.9 %all_to_all.31 = s16[64,9,2,128]{3,2,1,0:T(2,128)(2,1)S(1)} all-to-all(s16[64,9,2,128]{3,2,1,0:T(2,128)(2,1)S(1)} %bitcast.14), channel_id=1, replica_groups=mesh['prefix'=64,'tensor'=8] {'prefix'}, dimensions={0} | all-to-all | bytes 589824 | tf_op jit(solution)/shard_map/all_to_all | solution.py:331
  83.1 1.1 %combine.1 = bf16[8,8,1024]{2,1,0:T(8,128)(2,1)S(1)} custom-call(s32[65]{0:T(128)S(1)} %pad_add_fusion.slot_ref, s16[1152,128]{1,0:T(8,128)(2,1)S(1)} %bitcast.12, f32[64,8,128]{2,1,0:T(8,128)S(1)} %get-tuple-element.15.part_ref, f32[64,8,128]{2,1,0:T(8,128)S(1)} %get-tuple-element.16.lse_ref), custom_call_target="tpu_custom_call" | custom-call | tf_op jit(solution)/shard_map/combine/pallas_call | solution.py:294
  84.3 12.6 %all_to_all.32 = bf16[8,8,1024]{2,1,0:T(8,128)(2,1)S(1)} all-to-all(bf16[8,8,1024]{2,1,0:T(8,128)(2,1)S(1)} %combine.1), channel_id=1, replica_groups=mesh['prefix'=64,'tensor'=8] {'tensor'}, dimensions={0} | all-to-all | bytes 262144 | tf_op jit(solution)/shard_map/all_to_all | solution.py:335
  96.8 0.7 copy.8
  (1 shorter events, 0.0 us)
Async XLA Ops:
  0.0 15.4 %all-to-all-start = ((bf16[8,8,1024]{2,0,1:T(8,128)(2,1)}), bf16[8,8,1024]{2,0,1:T(8,128)(2,1)S(1)}, u32[]{:S(2)}, u32[]{:S(2)}) async-start(bf16[8,8,1024]{2,0,1:T(8,128)(2,1)} %bitcast.17), calls=%async_computation | async-start | bytes 262144 | tf_op jit(solution)/shard_map/all_to_all | solution.py:314
  16.7 33.5 %all-to-all-start.1 = ((bf16[64,16,128]{2,1,0:T(8,128)(2,1)}), bf16[64,16,128]{2,1,0:T(8,128)(2,1)S(1)}, u32[]{:S(2)}, u32[]{:S(2)}) async-start(bf16[64,16,128]{2,1,0:T(8,128)(2,1)} %bitcast.3), calls=%async_computation.1 | async-start | bytes 524288 | tf_op jit(solution)/shard_map/all_to_all | solution.py:326
  30.8 1.6 %copy-start = (bf16[64,2,1,64,128]{4,3,2,1,0:T(8,128)(2,1)S(1)}, bf16[64,2,1,64,128]{4,3,2,1,0:T(8,128)(2,1)}, u32[]{:S(2)}) copy-start(bf16[64,2,1,64,128]{4,3,2,1,0:T(8,128)(2,1)} %param.7) | copy-start | bytes 6291460
  32.4 1.6 %copy-start.1 = (bf16[1,2,1,4096,128]{4,3,2,1,0:T(8,128)(2,1)S(1)}, bf16[1,2,1,4096,128]{4,3,2,1,0:T(8,128)(2,1)}, u32[]{:S(2)}) copy-start(bf16[1,2,1,4096,128]{4,3,2,1,0:T(8,128)(2,1)} %prefix_ref.1) | copy-start | bytes 6291460
  34.0 0.7 copy-start.2

commit v3 on v2

--- a/solution.py
+++ b/solution.py
@@ -16,7 +16,7 @@
 SCORE_SCALE = math.log2(math.e) / math.sqrt(HD)
 
 BLOCK = 256
-CHUNK = 256
+CHUNK = 1024
 PAIRS = 8
 PAIR = SLOTS * GROUP
 SENT = PAIR + 2
@@ -109,8 +109,8 @@
 
     lax.fori_loop(0, pairs // PAIRS, body, 0)
     keys_ref[...] = prefix_ref[0, 0, 0]
-    for at in range(0, prefix_ref.shape[3], 2 * HD):
-        turned_ref[:, at : at + 2 * HD] = prefix_ref[0, 1, 0, at : at + 2 * HD, :].T
+    for k in range(turned_ref.shape[0]):
+        turned_ref[k] = prefix_ref[0, 1, 0, k * HD : (k + 1) * HD, :].T
 
 
 def suffix_attend(lengths, q_home, kv, prefix_kv):
@@ -120,7 +120,7 @@
     vmem = pl.BlockSpec(memory_space=pltpu.VMEM)
     return pl.pallas_call(
         suffix_kernel,
-        out_shape=(out, out, jax.ShapeDtypeStruct((prefix_kv.shape[3], HD), jnp.bfloat16), jax.ShapeDtypeStruct((HD, prefix_kv.shape[3]), jnp.bfloat16)),
+        out_shape=(out, out, jax.ShapeDtypeStruct((prefix_kv.shape[3], HD), jnp.bfloat16), jax.ShapeDtypeStruct((prefix_kv.shape[3] // HD, HD, HD), jnp.bfloat16)),
         in_specs=[pl.BlockSpec(memory_space=pltpu.SMEM), vmem, vmem, vmem],
         out_specs=(vmem, vmem, vmem, vmem),
         cost_estimate=pl.CostEstimate(
@@ -141,6 +141,10 @@
     blocks = rows // BLOCK
     chunks = span // CHUNK
     homes = HD // PAIR
+
+    def turned(at):
+        tiles = [vt_ref[k] for k in range(at // HD, (at + CHUNK) // HD)]
+        return jnp.concatenate(tiles, axis=1)
 
     def fold(x, op):
         return op(x.reshape(CHUNK // 8, 8, BLOCK), axis=0)
@@ -185,7 +189,7 @@
         if now is not None:
             shift = m_now[0:1, :]
             total = jnp.zeros((8, BLOCK), jnp.float32)
-            weighted = jnp.zeros((HD, BLOCK), jnp.float32)
+            weighted = [jnp.zeros((HD, BLOCK), jnp.float32)] * 2
         for c in range(chunks):
             at = c * CHUNK
             if ahead is not None:
@@ -197,8 +201,8 @@
             if now is not None:
                 w = jnp.exp2(s_now[at : at + CHUNK, :] * SCORE_SCALE - shift)
                 total = total + fold(w, jnp.sum)
-                weighted = weighted + jnp.dot(
-                    vt_ref[:, at : at + CHUNK],
+                weighted[c % 2] = weighted[c % 2] + jnp.dot(
+                    turned(at),
                     w.astype(jnp.bfloat16),
                     preferred_element_type=jnp.float32,
                 )
@@ -207,7 +211,7 @@
                 jnp.max(top, axis=0, keepdims=True) * SCORE_SCALE, (8, BLOCK)
             )
         if now is not None:
-            finish(now, weighted, jnp.sum(total, axis=0, keepdims=True), shift)
+            finish(now, weighted[0] + weighted[1], jnp.sum(total, axis=0, keepdims=True), shift)
 
     stage(0, s0_ref, m0_ref, None, None, None)
     for b in range(blocks - 1):

time: 97.9 us -> 97.4 us (level)
  no operation moved by 1% of the time
where the time goes in v3:
time: 97.4 us; the launch traced here: 97 us
  blocking collectives  39.5 us (41%)
  starting transfers between devices  24.2 us (25%)
  waiting for transfers between devices  17.2 us (18%)
  Pallas kernels  10.6 us (11%)
  local copies, waits for them, and re-layouts  4.49 us (5%)
  other arithmetic  0.99 us (1%)
    all_to_all x1, blocking collectives, on_device(): lax.all_to_all(packed.reshape(owners, SENT // 2, 2, HD), 'prefix', split_...  26.9 us
    all_to_all x1, starting transfers between devices, on_device(): lax.all_to_all(outgoing.reshape(owners, SLOTS * GROUP, HD), 'prefix', spl...  14.1 us
    all_to_all x1, waiting for transfers between devices, on_device(): lax.all_to_all(outgoing.reshape(owners, SLOTS * GROUP, HD), 'prefix', spl...  12.9 us
    all_to_all x1, blocking collectives, on_device(): lax.all_to_all(attended, 'tensor', split_axis=0, concat_axis=0, tiled=True)  12.6 us
    all_to_all x1, starting transfers between devices, on_device(): lax.all_to_all(queries, 'tensor', split_axis=1, concat_axis=0, tiled=True)  10.1 us
    pallas_call x1, Pallas kernels, prefix_attend(): pl.pallas_call(prefix_kernel, out_shape=jax.ShapeDtypeStruct((homes * SEN...  5.53 us
    unnamed x7, local copies, waits for them, and re-layouts  4.49 us
    all_to_all x1, waiting for transfers between devices, on_device(): lax.all_to_all(queries, 'tensor', split_axis=1, concat_axis=0, tiled=True)  4.26 us
  transfers between devices with their start and end apart: 2, of which 2 were waited for; matrix products, arithmetic and copies ran while one was open for 1% of the time, Pallas kernels for 3%

profile of v3, /device:TPU:1, one launch (start us, length us, event | category | flops | bytes accessed | tf_op | source)
XLA Modules:
  0.0 97.0 jit_solution(1622234767503071161)
XLA Ops:
  0.0 10.1 %all-to-all-start = ((bf16[8,8,1024]{2,0,1:T(8,128)(2,1)}), bf16[8,8,1024]{2,0,1:T(8,128)(2,1)S(1)}, u32[]{:S(2)}, u32[]{:S(2)}) async-start(bf16[8,8,1024]{2,0,1:T(8,128)(2,1)} %bitcast.17), calls=%async_computation | async-start | bytes 262144 | tf_op jit(solution)/shard_map/all_to_all | solution.py:318
  10.1 0.9 select_reduce_fusion
  11.0 0.1 pad_add_fusion.slot_ref
  11.1 4.3 %all-to-all-done = bf16[8,8,1024]{2,0,1:T(8,128)(2,1)S(1)} async-done(((bf16[8,8,1024]{2,0,1:T(8,128)(2,1)}), bf16[8,8,1024]{2,0,1:T(8,128)(2,1)S(1)}, u32[]{:S(2)}, u32[]{:S(2)}) %all-to-all-start) | async-done | bytes 131104 | tf_op jit(solution)/shard_map/all_to_all | solution.py:318
  15.4 1.3 %dispatch.1 = (bf16[128,8,128]{2,1,0:T(8,128)(2,1)}, bf16[32,16,128]{2,1,0:T(8,128)(2,1)S(1)}) custom-call(s32[65]{0:T(128)S(1)} %pad_add_fusion.slot_ref, bf16[8,8,1024]{2,1,0:T(8,128)(2,1)S(1)} %bitcast.13), custom_call_target="tpu_custom_call" | custom-call | tf_op jit(solution)/shard_map/dispatch/pallas_call | solution.py:48
  16.7 14.1 %all-to-all-start.1 = ((bf16[64,16,128]{2,1,0:T(8,128)(2,1)}), bf16[64,16,128]{2,1,0:T(8,128)(2,1)S(1)}, u32[]{:S(2)}, u32[]{:S(2)}) async-start(bf16[64,16,128]{2,1,0:T(8,128)(2,1)} %bitcast.3), calls=%async_computation.1 | async-start | bytes 524288 | tf_op jit(solution)/shard_map/all_to_all | solution.py:330
  30.8 0.0 copy-start
  30.8 1.6 %copy-done = bf16[64,2,1,64,128]{4,3,2,1,0:T(8,128)(2,1)S(1)} copy-done((bf16[64,2,1,64,128]{4,3,2,1,0:T(8,128)(2,1)S(1)}, bf16[64,2,1,64,128]{4,3,2,1,0:T(8,128)(2,1)}, u32[]{:S(2)}) %copy-start) | copy-done | bytes 2097176
  32.4 0.0 copy-start.1
  32.4 1.6 %copy-done.1 = bf16[1,2,1,4096,128]{4,3,2,1,0:T(8,128)(2,1)S(1)} copy-done((bf16[1,2,1,4096,128]{4,3,2,1,0:T(8,128)(2,1)S(1)}, bf16[1,2,1,4096,128]{4,3,2,1,0:T(8,128)(2,1)}, u32[]{:S(2)}) %copy-start.1) | copy-done | bytes 2097176
  34.0 0.0 copy-start.2
  34.0 0.7 copy-done.2
  34.6 2.6 %suffix_attend.1 = (f32[64,8,128]{2,1,0:T(8,128)S(1)}, f32[64,8,128]{2,1,0:T(8,128)S(1)}, bf16[4096,128]{1,0:T(8,128)(2,1)S(1)}, bf16[32,128,128]{2,1,0:T(8,128)(2,1)S(1)}) custom-call(s32[64]{0:T(128)S(1)} %copy-done.2, bf16[32,16,128]{2,1,0:T(8,128)(2,1)S(1)} %get-tuple-element.12.q_ref, bf16[64,2,64,128]{3,2,1,0:T(8,128)(2,1)S(1)} %bitcast.11, ...), custom_call_target="tpu_custom_call" | custom-call | flops 16777216 | bytes 4194304 | tf_op jit(solution)/shard_map/suffix_attend/pallas_call | solution.py:121
  37.3 12.9 %all-to-all-done.1 = bf16[64,16,128]{2,1,0:T(8,128)(2,1)S(1)} async-done(((bf16[64,16,128]{2,1,0:T(8,128)(2,1)}), bf16[64,16,128]{2,1,0:T(8,128)(2,1)S(1)}, u32[]{:S(2)}, u32[]{:S(2)}) %all-to-all-start.1) | async-done | bytes 262176 | tf_op jit(solution)/shard_map/all_to_all | solution.py:330
  50.2 5.5 %prefix_attend.1 = s16[1152,128]{1,0:T(8,128)(2,1)S(1)} custom-call(bf16[1024,128]{1,0:T(8,128)(2,1)S(1)} %bitcast.15, bf16[4096,128]{1,0:T(8,128)(2,1)S(1)} %get-tuple-element.13.k_ref, bf16[32,128,128]{2,1,0:T(8,128)(2,1)S(1)} %get-tuple-element.14.vt_ref), custom_call_target="tpu_custom_call" | custom-call | flops 2147483648 | bytes 2097152 | tf_op jit(solution)/shard_map/prefix_attend/pallas_call | solution.py:231
  55.7 26.9 %all_to_all.31 = s16[64,9,2,128]{3,2,1,0:T(2,128)(2,1)S(1)} all-to-all(s16[64,9,2,128]{3,2,1,0:T(2,128)(2,1)S(1)} %bitcast.14), channel_id=1, replica_groups=mesh['prefix'=64,'tensor'=8] {'prefix'}, dimensions={0} | all-to-all | bytes 589824 | tf_op jit(solution)/shard_map/all_to_all | solution.py:335
  82.6 1.1 %combine.1 = bf16[8,8,1024]{2,1,0:T(8,128)(2,1)S(1)} custom-call(s32[65]{0:T(128)S(1)} %pad_add_fusion.slot_ref, s16[1152,128]{1,0:T(8,128)(2,1)S(1)} %bitcast.12, f32[64,8,128]{2,1,0:T(8,128)S(1)} %get-tuple-element.15.part_ref, f32[64,8,128]{2,1,0:T(8,128)S(1)} %get-tuple-element.16.lse_ref), custom_call_target="tpu_custom_call" | custom-call | tf_op jit(solution)/shard_map/combine/pallas_call | solution.py:298
  83.8 12.6 %all_to_all.32 = bf16[8,8,1024]{2,1,0:T(8,128)(2,1)S(1)} all-to-all(bf16[8,8,1024]{2,1,0:T(8,128)(2,1)S(1)} %combine.1), channel_id=1, replica_groups=mesh['prefix'=64,'tensor'=8] {'tensor'}, dimensions={0} | all-to-all | bytes 262144 | tf_op jit(solution)/shard_map/all_to_all | solution.py:339
  96.3 0.7 copy.8
  (1 shorter events, 0.0 us)
Async XLA Ops:
  0.0 15.4 %all-to-all-start = ((bf16[8,8,1024]{2,0,1:T(8,128)(2,1)}), bf16[8,8,1024]{2,0,1:T(8,128)(2,1)S(1)}, u32[]{:S(2)}, u32[]{:S(2)}) async-start(bf16[8,8,1024]{2,0,1:T(8,128)(2,1)} %bitcast.17), calls=%async_computation | async-start | bytes 262144 | tf_op jit(solution)/shard_map/all_to_all | solution.py:318
  16.7 33.5 %all-to-all-start.1 = ((bf16[64,16,128]{2,1,0:T(8,128)(2,1)}), bf16[64,16,128]{2,1,0:T(8,128)(2,1)S(1)}, u32[]{:S(2)}, u32[]{:S(2)}) async-start(bf16[64,16,128]{2,1,0:T(8,128)(2,1)} %bitcast.3), calls=%async_computation.1 | async-start | bytes 524288 | tf_op jit(solution)/shard_map/all_to_all | solution.py:330
  30.8 1.6 %copy-start = (bf16[64,2,1,64,128]{4,3,2,1,0:T(8,128)(2,1)S(1)}, bf16[64,2,1,64,128]{4,3,2,1,0:T(8,128)(2,1)}, u32[]{:S(2)}) copy-start(bf16[64,2,1,64,128]{4,3,2,1,0:T(8,128)(2,1)} %param.7) | copy-start | bytes 6291460
  32.4 1.6 %copy-start.1 = (bf16[1,2,1,4096,128]{4,3,2,1,0:T(8,128)(2,1)S(1)}, bf16[1,2,1,4096,128]{4,3,2,1,0:T(8,128)(2,1)}, u32[]{:S(2)}) copy-start(bf16[1,2,1,4096,128]{4,3,2,1,0:T(8,128)(2,1)} %prefix_ref.1) | copy-start | bytes 6291460
  34.0 0.7 copy-start.2

commit v4 on v3

--- a/solution.py
+++ b/solution.py
@@ -18,51 +18,62 @@
 BLOCK = 256
 CHUNK = 1024
 PAIRS = 8
+PARTS = 4
 PAIR = SLOTS * GROUP
 SENT = PAIR + 2
 
 NT = (((1,), (1,)), ((), ()))
 
 
-def dispatch_kernel(slot_ref, q_ref, out_ref, home_ref, tile_ref):
+def dispatch_kernel(table_ref, q_ref, out_ref, home_ref, tile_ref, stage_ref, sems):
     tensor, rows, width = q_ref.shape
+    count = tensor * rows
     for t in range(tensor):
         for h in range(GROUP):
             tile_ref[pl.ds((t * GROUP + h) * rows, rows), :] = q_ref[
                 t, :, h * HD : (h + 1) * HD
             ].astype(jnp.float32)
-    for r in range(0, tensor * rows, 2):
+    slots = stage_ref.shape[0]
+    size = slots // PARTS
+    copies = []
+    for part in range(PARTS):
+        for s in range(part * size, (part + 1) * size):
+            first = table_ref[count + 1 + s]
+            tile = tile_ref[pl.ds(first, GROUP, stride=rows), :]
+            stage_ref[s] = tile.astype(jnp.bfloat16)
+        at = pl.ds(part * size, size)
+        copies.append(pltpu.make_async_copy(stage_ref.at[at], out_ref.at[at], sems.at[part]))
+        copies[part].start()
+    for r in range(0, count, 2):
         pair = []
         for k in range(2):
             t, i = divmod(r + k, rows)
-            tile = tile_ref[pl.ds(t * GROUP * rows + i, GROUP, stride=rows), :]
-            pair.append(tile)
-            out_ref[slot_ref[r + k]] = tile.astype(jnp.bfloat16)
+            pair.append(tile_ref[pl.ds(t * GROUP * rows + i, GROUP, stride=rows), :])
         home_ref[r // 2] = jnp.concatenate(pair, axis=0).astype(jnp.bfloat16)
-
-
-def dispatch(slot, q_rows):
+    for part in range(PARTS):
+        copies[part].wait()
+
+
+def dispatch(table, q_rows, slots):
     tensor, rows, width = q_rows.shape
     count = tensor * rows
-    owners = count
+    vmem = pl.BlockSpec(memory_space=pltpu.VMEM)
     return pl.pallas_call(
         dispatch_kernel,
         out_shape=(
-            jax.ShapeDtypeStruct((owners * SLOTS, GROUP, HD), jnp.bfloat16),
+            jax.ShapeDtypeStruct((slots, GROUP, HD), jnp.bfloat16),
             jax.ShapeDtypeStruct((count // 2, 2 * GROUP, HD), jnp.bfloat16),
         ),
-        in_specs=[
-            pl.BlockSpec(memory_space=pltpu.SMEM),
-            pl.BlockSpec(memory_space=pltpu.VMEM),
+        in_specs=[pl.BlockSpec(memory_space=pltpu.SMEM), vmem],
+        out_specs=(pl.BlockSpec(memory_space=pltpu.HBM), vmem),
+        scratch_shapes=[
+            pltpu.VMEM((count * GROUP, HD), jnp.float32),
+            pltpu.VMEM((slots, GROUP, HD), jnp.bfloat16),
+            pltpu.SemaphoreType.DMA((PARTS,)),
         ],
-        out_specs=(
-            pl.BlockSpec(memory_space=pltpu.VMEM),
-            pl.BlockSpec(memory_space=pltpu.VMEM),
-        ),
-        scratch_shapes=[pltpu.VMEM((count * GROUP, HD), jnp.float32)],
         compiler_params=pltpu.CompilerParams(vmem_limit_bytes=8 << 20),
         name="dispatch",
-    )(slot, q_rows)
+    )(table, q_rows)
 
 
 def suffix_kernel(length_ref, q_ref, kv_ref, prefix_ref, part_ref, lse_ref, keys_ref, turned_ref):
@@ -250,19 +261,19 @@
 
 
 def combine_kernel(
-    slot_ref, back_ref, part_ref, lse_ref, out_ref, back32_ref, tile_ref
+    table_ref, back_ref, part_ref, lse_ref, out_ref, back32_ref, tile_ref
 ):
     tensor, rows, width = out_ref.shape
     lane = lax.broadcasted_iota(jnp.int32, (GROUP, HD), 1)
     head = lax.broadcasted_iota(jnp.int32, (GROUP, HD), 0)
-    own = (slot_ref[tensor * rows] % (HD // PAIR)) * PAIR
+    own = (table_ref[tensor * rows] % (HD // PAIR)) * PAIR
     own_step = (own + HD // 2) % HD
     for k in range(0, back_ref.shape[0], 16):
         back32_ref[k : k + 16, :] = back_ref[k : k + 16, :].astype(jnp.int32).astype(jnp.float32)
     for t in range(tensor):
         for i in range(rows):
             r = t * rows + i
-            slot = slot_ref[r]
+            slot = table_ref[r]
             base = (slot // SLOTS) * SENT
             inner = (slot % SLOTS) * GROUP
             upper = back32_ref[pl.ds(base + PAIR, 1), :]
@@ -291,8 +302,8 @@
             ].astype(jnp.bfloat16)
 
 
-def combine(slot, back, suffix, tensor):
-    count = slot.shape[0] - 1
+def combine(table, back, suffix, tensor):
+    count = suffix[0].shape[0]
     vmem = pl.BlockSpec(memory_space=pltpu.VMEM)
     smem = pl.BlockSpec(memory_space=pltpu.SMEM)
     return pl.pallas_call(
@@ -306,7 +317,7 @@
         ],
         compiler_params=pltpu.CompilerParams(vmem_limit_bytes=8 << 20),
         name="combine",
-    )(slot, back, *suffix)
+    )(table, back, *suffix)
 
 
 def on_device(queries, suffix_kv, suffix_lengths, prefix_kv, tree_ids, owner_map):
@@ -325,8 +336,11 @@
     slot = owner_row * SLOTS + jnp.sum(earlier.astype(jnp.int32), axis=1)
 
     home = lax.axis_index("prefix").astype(jnp.int32)
-    slot = jnp.concatenate([slot, home.reshape(1)])
-    outgoing, q_home = dispatch(slot, q_rows)
+    first = (place // rows) * (GROUP * rows) + place % rows
+    slots = jnp.arange(owners * SLOTS, dtype=jnp.int32)
+    pick = jnp.sum(jnp.where(slots[:, None] == slot[None, :], first[None, :], 0), axis=1)
+    table = jnp.concatenate([slot, home.reshape(1), pick])
+    outgoing, q_home = dispatch(table, q_rows, owners * SLOTS)
     arrived = lax.all_to_all(
         outgoing.reshape(owners, SLOTS * GROUP, HD), "prefix", split_axis=0, concat_axis=0, tiled=True
     )
@@ -335,7 +349,7 @@
     back = lax.all_to_all(
         packed.reshape(owners, SENT // 2, 2, HD), "prefix", split_axis=0, concat_axis=0, tiled=True
     )
-    attended = combine(slot, back.reshape(owners * SENT, HD), suffix, tensor)
+    attended = combine(table, back.reshape(owners * SENT, HD), suffix, tensor)
     done = lax.all_to_all(attended, "tensor", split_axis=0, concat_axis=0, tiled=True)
     return jnp.swapaxes(done, 0, 1).reshape(rows, tensor * width)
 

time: 97.4 us -> 97.5 us (level)
  no operation moved by 1% of the time
where the time goes in v4:
time: 97.5 us; the launch traced here: 97.1 us
  blocking collectives  39.5 us (41%)
  starting transfers between devices  24.2 us (25%)
  waiting for transfers between devices  17.1 us (18%)
  Pallas kernels  10.7 us (11%)
  local copies, waits for them, and re-layouts  4.49 us (5%)
  other arithmetic  1.1 us (1%)
    all_to_all x1, blocking collectives, on_device(): lax.all_to_all(packed.reshape(owners, SENT // 2, 2, HD), 'prefix', split_...  26.9 us
    all_to_all x1, starting transfers between devices, on_device(): lax.all_to_all(outgoing.reshape(owners, SLOTS * GROUP, HD), 'prefix', spl...  14.1 us
    all_to_all x1, waiting for transfers between devices, on_device(): lax.all_to_all(outgoing.reshape(owners, SLOTS * GROUP, HD), 'prefix', spl...  12.9 us
    all_to_all x1, blocking collectives, on_device(): lax.all_to_all(attended, 'tensor', split_axis=0, concat_axis=0, tiled=True)  12.6 us
    all_to_all x1, starting transfers between devices, on_device(): lax.all_to_all(queries, 'tensor', split_axis=1, concat_axis=0, tiled=True)  10.1 us
    pallas_call x1, Pallas kernels, prefix_attend(): pl.pallas_call(prefix_kernel, out_shape=jax.ShapeDtypeStruct((homes * SEN...  5.53 us
    unnamed x7, local copies, waits for them, and re-layouts  4.49 us
    all_to_all x1, waiting for transfers between devices, on_device(): lax.all_to_all(queries, 'tensor', split_axis=1, concat_axis=0, tiled=True)  4.15 us
  transfers between devices with their start and end apart: 2, of which 2 were waited for; matrix products, arithmetic and copies ran while one was open for 1% of the time, Pallas kernels for 3%

profile of v4, /device:TPU:1, one launch (start us, length us, event | category | flops | bytes accessed | tf_op | source)
XLA Modules:
  0.0 97.1 jit_solution(14248134708579006797)
XLA Ops:
  0.0 10.1 %all-to-all-start = ((bf16[8,8,1024]{2,0,1:T(8,128)(2,1)}), bf16[8,8,1024]{2,0,1:T(8,128)(2,1)S(1)}, u32[]{:S(2)}, u32[]{:S(2)}) async-start(bf16[8,8,1024]{2,0,1:T(8,128)(2,1)} %bitcast.17), calls=%async_computation | async-start | bytes 262144 | tf_op jit(solution)/shard_map/all_to_all | solution.py:329
  10.1 0.9 select_reduce_fusion.1
  11.0 0.1 select_reduce_fusion
  11.1 0.1 pad_add_fusion.table_ref
  11.2 4.2 %all-to-all-done = bf16[8,8,1024]{2,0,1:T(8,128)(2,1)S(1)} async-done(((bf16[8,8,1024]{2,0,1:T(8,128)(2,1)}), bf16[8,8,1024]{2,0,1:T(8,128)(2,1)S(1)}, u32[]{:S(2)}, u32[]{:S(2)}) %all-to-all-start) | async-done | bytes 131104 | tf_op jit(solution)/shard_map/all_to_all | solution.py:329
  15.4 1.4 %dispatch.1 = (bf16[128,8,128]{2,1,0:T(8,128)(2,1)}, bf16[32,16,128]{2,1,0:T(8,128)(2,1)S(1)}) custom-call(s32[193]{0:T(256)S(1)} %pad_add_fusion.table_ref, bf16[8,8,1024]{2,1,0:T(8,128)(2,1)S(1)} %bitcast.13), custom_call_target="tpu_custom_call" | custom-call | tf_op jit(solution)/shard_map/dispatch/pallas_call | solution.py:61
  16.8 14.1 %all-to-all-start.1 = ((bf16[64,16,128]{2,1,0:T(8,128)(2,1)}), bf16[64,16,128]{2,1,0:T(8,128)(2,1)S(1)}, u32[]{:S(2)}, u32[]{:S(2)}) async-start(bf16[64,16,128]{2,1,0:T(8,128)(2,1)} %bitcast.3), calls=%async_computation.1 | async-start | bytes 524288 | tf_op jit(solution)/shard_map/all_to_all | solution.py:344
  30.9 0.0 copy-start
  30.9 1.6 %copy-done = bf16[64,2,1,64,128]{4,3,2,1,0:T(8,128)(2,1)S(1)} copy-done((bf16[64,2,1,64,128]{4,3,2,1,0:T(8,128)(2,1)S(1)}, bf16[64,2,1,64,128]{4,3,2,1,0:T(8,128)(2,1)}, u32[]{:S(2)}) %copy-start) | copy-done | bytes 2097176
  32.5 0.0 copy-start.1
  32.5 1.6 %copy-done.1 = bf16[1,2,1,4096,128]{4,3,2,1,0:T(8,128)(2,1)S(1)} copy-done((bf16[1,2,1,4096,128]{4,3,2,1,0:T(8,128)(2,1)S(1)}, bf16[1,2,1,4096,128]{4,3,2,1,0:T(8,128)(2,1)}, u32[]{:S(2)}) %copy-start.1) | copy-done | bytes 2097176
  34.1 0.0 copy-start.2
  34.1 0.7 copy-done.2
  34.7 2.6 %suffix_attend.1 = (f32[64,8,128]{2,1,0:T(8,128)S(1)}, f32[64,8,128]{2,1,0:T(8,128)S(1)}, bf16[4096,128]{1,0:T(8,128)(2,1)S(1)}, bf16[32,128,128]{2,1,0:T(8,128)(2,1)S(1)}) custom-call(s32[64]{0:T(128)S(1)} %copy-done.2, bf16[32,16,128]{2,1,0:T(8,128)(2,1)S(1)} %get-tuple-element.12.q_ref, bf16[64,2,64,128]{3,2,1,0:T(8,128)(2,1)S(1)} %bitcast.11, ...), custom_call_target="tpu_custom_call" | custom-call | flops 16777216 | bytes 4194304 | tf_op jit(solution)/shard_map/suffix_attend/pallas_call | solution.py:132
  37.4 12.9 %all-to-all-done.1 = bf16[64,16,128]{2,1,0:T(8,128)(2,1)S(1)} async-done(((bf16[64,16,128]{2,1,0:T(8,128)(2,1)}), bf16[64,16,128]{2,1,0:T(8,128)(2,1)S(1)}, u32[]{:S(2)}, u32[]{:S(2)}) %all-to-all-start.1) | async-done | bytes 262176 | tf_op jit(solution)/shard_map/all_to_all | solution.py:344
  50.3 5.5 %prefix_attend.1 = s16[1152,128]{1,0:T(8,128)(2,1)S(1)} custom-call(bf16[1024,128]{1,0:T(8,128)(2,1)S(1)} %bitcast.15, bf16[4096,128]{1,0:T(8,128)(2,1)S(1)} %get-tuple-element.13.k_ref, bf16[32,128,128]{2,1,0:T(8,128)(2,1)S(1)} %get-tuple-element.14.vt_ref), custom_call_target="tpu_custom_call" | custom-call | flops 2147483648 | bytes 2097152 | tf_op jit(solution)/shard_map/prefix_attend/pallas_call | solution.py:242
  55.8 26.9 %all_to_all.31 = s16[64,9,2,128]{3,2,1,0:T(2,128)(2,1)S(1)} all-to-all(s16[64,9,2,128]{3,2,1,0:T(2,128)(2,1)S(1)} %bitcast.14), channel_id=1, replica_groups=mesh['prefix'=64,'tensor'=8] {'prefix'}, dimensions={0} | all-to-all | bytes 589824 | tf_op jit(solution)/shard_map/all_to_all | solution.py:349
  82.7 1.1 %combine.1 = bf16[8,8,1024]{2,1,0:T(8,128)(2,1)S(1)} custom-call(s32[193]{0:T(256)S(1)} %pad_add_fusion.table_ref, s16[1152,128]{1,0:T(8,128)(2,1)S(1)} %bitcast.12, f32[64,8,128]{2,1,0:T(8,128)S(1)} %get-tuple-element.15.part_ref, f32[64,8,128]{2,1,0:T(8,128)S(1)} %get-tuple-element.16.lse_ref), custom_call_target="tpu_custom_call" | custom-call | tf_op jit(solution)/shard_map/combine/pallas_call | solution.py:309
  83.9 12.6 %all_to_all.32 = bf16[8,8,1024]{2,1,0:T(8,128)(2,1)S(1)} all-to-all(bf16[8,8,1024]{2,1,0:T(8,128)(2,1)S(1)} %combine.1), channel_id=1, replica_groups=mesh['prefix'=64,'tensor'=8] {'tensor'}, dimensions={0} | all-to-all | bytes 262144 | tf_op jit(solution)/shard_map/all_to_all | solution.py:353
  96.4 0.7 copy.8
  (2 shorter events, 0.0 us)
Async XLA Ops:
  0.0 15.4 %all-to-all-start = ((bf16[8,8,1024]{2,0,1:T(8,128)(2,1)}), bf16[8,8,1024]{2,0,1:T(8,128)(2,1)S(1)}, u32[]{:S(2)}, u32[]{:S(2)}) async-start(bf16[8,8,1024]{2,0,1:T(8,128)(2,1)} %bitcast.17), calls=%async_computation | async-start | bytes 262144 | tf_op jit(solution)/shard_map/all_to_all | solution.py:329
  16.8 33.5 %all-to-all-start.1 = ((bf16[64,16,128]{2,1,0:T(8,128)(2,1)}), bf16[64,16,128]{2,1,0:T(8,128)(2,1)S(1)}, u32[]{:S(2)}, u32[]{:S(2)}) async-start(bf16[64,16,128]{2,1,0:T(8,128)(2,1)} %bitcast.3), calls=%async_computation.1 | async-start | bytes 524288 | tf_op jit(solution)/shard_map/all_to_all | solution.py:344
  30.9 1.6 %copy-start = (bf16[64,2,1,64,128]{4,3,2,1,0:T(8,128)(2,1)S(1)}, bf16[64,2,1,64,128]{4,3,2,1,0:T(8,128)(2,1)}, u32[]{:S(2)}) copy-start(bf16[64,2,1,64,128]{4,3,2,1,0:T(8,128)(2,1)} %param.7) | copy-start | bytes 6291460
  32.5 1.6 %copy-start.1 = (bf16[1,2,1,4096,128]{4,3,2,1,0:T(8,128)(2,1)S(1)}, bf16[1,2,1,4096,128]{4,3,2,1,0:T(8,128)(2,1)}, u32[]{:S(2)}) copy-start(bf16[1,2,1,4096,128]{4,3,2,1,0:T(8,128)(2,1)} %prefix_ref.1) | copy-start | bytes 6291460
  34.1 0.7 copy-start.2

commit v5 on v4

--- a/solution.py
+++ b/solution.py
@@ -25,7 +25,11 @@
 NT = (((1,), (1,)), ((), ()))
 
 
-def dispatch_kernel(table_ref, q_ref, out_ref, home_ref, tile_ref, stage_ref, sems):
+def dispatch_kernel(
+    table_in_ref, q_ref, out_ref, home_ref, tile_ref, stage_ref, sems, table_ref, table_sem
+):
+    table_copy = pltpu.make_async_copy(table_in_ref, table_ref, table_sem)
+    table_copy.start()
     tensor, rows, width = q_ref.shape
     count = tensor * rows
     for t in range(tensor):
@@ -33,6 +37,7 @@
             tile_ref[pl.ds((t * GROUP + h) * rows, rows), :] = q_ref[
                 t, :, h * HD : (h + 1) * HD
             ].astype(jnp.float32)
+    table_copy.wait()
     slots = stage_ref.shape[0]
     size = slots // PARTS
     copies = []
@@ -64,12 +69,14 @@
             jax.ShapeDtypeStruct((slots, GROUP, HD), jnp.bfloat16),
             jax.ShapeDtypeStruct((count // 2, 2 * GROUP, HD), jnp.bfloat16),
         ),
-        in_specs=[pl.BlockSpec(memory_space=pltpu.SMEM), vmem],
+        in_specs=[pl.BlockSpec(memory_space=pl.ANY), vmem],
         out_specs=(pl.BlockSpec(memory_space=pltpu.HBM), vmem),
         scratch_shapes=[
             pltpu.VMEM((count * GROUP, HD), jnp.float32),
             pltpu.VMEM((slots, GROUP, HD), jnp.bfloat16),
             pltpu.SemaphoreType.DMA((PARTS,)),
+            pltpu.SMEM(table.shape, jnp.int32),
+            pltpu.SemaphoreType.DMA,
         ],
         compiler_params=pltpu.CompilerParams(vmem_limit_bytes=8 << 20),
         name="dispatch",
@@ -261,15 +268,18 @@
 
 
 def combine_kernel(
-    table_ref, back_ref, part_ref, lse_ref, out_ref, back32_ref, tile_ref
+    table_in_ref, back_ref, part_ref, lse_ref, out_ref, back32_ref, tile_ref, table_ref, table_sem
 ):
+    table_copy = pltpu.make_async_copy(table_in_ref, table_ref, table_sem)
+    table_copy.start()
     tensor, rows, width = out_ref.shape
     lane = lax.broadcasted_iota(jnp.int32, (GROUP, HD), 1)
     head = lax.broadcasted_iota(jnp.int32, (GROUP, HD), 0)
+    for k in range(0, back_ref.shape[0], 16):
+        back32_ref[k : k + 16, :] = back_ref[k : k + 16, :].astype(jnp.int32).astype(jnp.float32)
+    table_copy.wait()
     own = (table_ref[tensor * rows] % (HD // PAIR)) * PAIR
     own_step = (own + HD // 2) % HD
-    for k in range(0, back_ref.shape[0], 16):
-        back32_ref[k : k + 16, :] = back_ref[k : k + 16, :].astype(jnp.int32).astype(jnp.float32)
     for t in range(tensor):
         for i in range(rows):
             r = t * rows + i
@@ -305,15 +315,16 @@
 def combine(table, back, suffix, tensor):
     count = suffix[0].shape[0]
     vmem = pl.BlockSpec(memory_space=pltpu.VMEM)
-    smem = pl.BlockSpec(memory_space=pltpu.SMEM)
     return pl.pallas_call(
         combine_kernel,
         out_shape=jax.ShapeDtypeStruct((tensor, count // tensor, GROUP * HD), jnp.bfloat16),
-        in_specs=[smem] + [vmem] * 3,
+        in_specs=[pl.BlockSpec(memory_space=pl.ANY)] + [vmem] * 3,
         out_specs=vmem,
         scratch_shapes=[
             pltpu.VMEM(back.shape, jnp.float32),
             pltpu.VMEM((count * GROUP, HD), jnp.float32),
+            pltpu.SMEM(table.shape, jnp.int32),
+            pltpu.SemaphoreType.DMA,
         ],
         compiler_params=pltpu.CompilerParams(vmem_limit_bytes=8 << 20),
         name="combine",
@@ -340,6 +351,7 @@
     slots = jnp.arange(owners * SLOTS, dtype=jnp.int32)
     pick = jnp.sum(jnp.where(slots[:, None] == slot[None, :], first[None, :], 0), axis=1)
     table = jnp.concatenate([slot, home.reshape(1), pick])
+    table = jnp.pad(table, (0, -table.shape[0] % (2 * HD)))
     outgoing, q_home = dispatch(table, q_rows, owners * SLOTS)
     arrived = lax.all_to_all(
         outgoing.reshape(owners, SLOTS * GROUP, HD), "prefix", split_axis=0, concat_axis=0, tiled=True

time: 97.5 us -> 97.5 us (level)
  no operation moved by 1% of the time
where the time goes in v5:
time: 97.5 us; the launch traced here: 97.1 us
  blocking collectives  39.4 us (40%)
  starting transfers between devices  24.2 us (25%)
  waiting for transfers between devices  17.1 us (18%)
  Pallas kernels  10.7 us (11%)
  local copies, waits for them, and re-layouts  4.49 us (5%)
  other arithmetic  1.09 us (1%)
    all_to_all x1, blocking collectives, on_device(): lax.all_to_all(packed.reshape(owners, SENT // 2, 2, HD), 'prefix', split_...  26.9 us
    all_to_all x1, starting transfers between devices, on_device(): lax.all_to_all(outgoing.reshape(owners, SLOTS * GROUP, HD), 'prefix', spl...  14.1 us
    all_to_all x1, waiting for transfers between devices, on_device(): lax.all_to_all(outgoing.reshape(owners, SLOTS * GROUP, HD), 'prefix', spl...  12.9 us
    all_to_all x1, blocking collectives, on_device(): lax.all_to_all(attended, 'tensor', split_axis=0, concat_axis=0, tiled=True)  12.6 us
    all_to_all x1, starting transfers between devices, on_device(): lax.all_to_all(queries, 'tensor', split_axis=1, concat_axis=0, tiled=True)  10.1 us
    pallas_call x1, Pallas kernels, prefix_attend(): pl.pallas_call(prefix_kernel, out_shape=jax.ShapeDtypeStruct((homes * SEN...  5.54 us
    unnamed x7, local copies, waits for them, and re-layouts  4.49 us
    all_to_all x1, waiting for transfers between devices, on_device(): lax.all_to_all(queries, 'tensor', split_axis=1, concat_axis=0, tiled=True)  4.15 us
  transfers between devices with their start and end apart: 2, of which 2 were waited for; matrix products, arithmetic and copies ran while one was open for 1% of the time, Pallas kernels for 3%

profile of v5, /device:TPU:1, one launch (start us, length us, event | category | flops | bytes accessed | tf_op | source)
XLA Modules:
  0.0 97.1 jit_solution(14516983042157301689)
XLA Ops:
  0.0 10.1 %all-to-all-start = ((bf16[8,8,1024]{2,0,1:T(8,128)(2,1)}), bf16[8,8,1024]{2,0,1:T(8,128)(2,1)S(1)}, u32[]{:S(2)}, u32[]{:S(2)}) async-start(bf16[8,8,1024]{2,0,1:T(8,128)(2,1)} %bitcast.17), calls=%async_computation | async-start | bytes 262144 | tf_op jit(solution)/shard_map/all_to_all | solution.py:340
  10.1 0.9 select_reduce_fusion.1
  11.0 0.1 select_reduce_fusion
  11.1 0.1 pad_add_fusion
  11.2 4.2 %all-to-all-done = bf16[8,8,1024]{2,0,1:T(8,128)(2,1)S(1)} async-done(((bf16[8,8,1024]{2,0,1:T(8,128)(2,1)}), bf16[8,8,1024]{2,0,1:T(8,128)(2,1)S(1)}, u32[]{:S(2)}, u32[]{:S(2)}) %all-to-all-start) | async-done | bytes 131104 | tf_op jit(solution)/shard_map/all_to_all | solution.py:340
  15.4 1.4 %dispatch.1 = (bf16[128,8,128]{2,1,0:T(8,128)(2,1)}, bf16[32,16,128]{2,1,0:T(8,128)(2,1)S(1)}) custom-call(s32[256]{0:T(256)S(1)} %pad.4.table_in_ref, bf16[8,8,1024]{2,1,0:T(8,128)(2,1)S(1)} %bitcast.13), custom_call_target="tpu_custom_call" | custom-call | tf_op jit(solution)/shard_map/dispatch/pallas_call | solution.py:66
  16.7 14.1 %all-to-all-start.1 = ((bf16[64,16,128]{2,1,0:T(8,128)(2,1)}), bf16[64,16,128]{2,1,0:T(8,128)(2,1)S(1)}, u32[]{:S(2)}, u32[]{:S(2)}) async-start(bf16[64,16,128]{2,1,0:T(8,128)(2,1)} %bitcast.3), calls=%async_computation.1 | async-start | bytes 524288 | tf_op jit(solution)/shard_map/all_to_all | solution.py:356
  30.9 0.0 copy-start
  30.9 1.6 %copy-done = bf16[64,2,1,64,128]{4,3,2,1,0:T(8,128)(2,1)S(1)} copy-done((bf16[64,2,1,64,128]{4,3,2,1,0:T(8,128)(2,1)S(1)}, bf16[64,2,1,64,128]{4,3,2,1,0:T(8,128)(2,1)}, u32[]{:S(2)}) %copy-start) | copy-done | bytes 2097176
  32.5 0.0 copy-start.1
  32.5 1.6 %copy-done.1 = bf16[1,2,1,4096,128]{4,3,2,1,0:T(8,128)(2,1)S(1)} copy-done((bf16[1,2,1,4096,128]{4,3,2,1,0:T(8,128)(2,1)S(1)}, bf16[1,2,1,4096,128]{4,3,2,1,0:T(8,128)(2,1)}, u32[]{:S(2)}) %copy-start.1) | copy-done | bytes 2097176
  34.1 0.0 copy-start.2
  34.1 0.7 copy-done.2
  34.7 2.6 %suffix_attend.1 = (f32[64,8,128]{2,1,0:T(8,128)S(1)}, f32[64,8,128]{2,1,0:T(8,128)S(1)}, bf16[4096,128]{1,0:T(8,128)(2,1)S(1)}, bf16[32,128,128]{2,1,0:T(8,128)(2,1)S(1)}) custom-call(s32[64]{0:T(128)S(1)} %copy-done.2, bf16[32,16,128]{2,1,0:T(8,128)(2,1)S(1)} %get-tuple-element.12.q_ref, bf16[64,2,64,128]{3,2,1,0:T(8,128)(2,1)S(1)} %bitcast.11, ...), custom_call_target="tpu_custom_call" | custom-call | flops 16777216 | bytes 4194304 | tf_op jit(solution)/shard_map/suffix_attend/pallas_call | solution.py:139
  37.4 12.9 %all-to-all-done.1 = bf16[64,16,128]{2,1,0:T(8,128)(2,1)S(1)} async-done(((bf16[64,16,128]{2,1,0:T(8,128)(2,1)}), bf16[64,16,128]{2,1,0:T(8,128)(2,1)S(1)}, u32[]{:S(2)}, u32[]{:S(2)}) %all-to-all-start.1) | async-done | bytes 262176 | tf_op jit(solution)/shard_map/all_to_all | solution.py:356
  50.3 5.5 %prefix_attend.1 = s16[1152,128]{1,0:T(8,128)(2,1)S(1)} custom-call(bf16[1024,128]{1,0:T(8,128)(2,1)S(1)} %bitcast.15, bf16[4096,128]{1,0:T(8,128)(2,1)S(1)} %get-tuple-element.13.k_ref, bf16[32,128,128]{2,1,0:T(8,128)(2,1)S(1)} %get-tuple-element.14.vt_ref), custom_call_target="tpu_custom_call" | custom-call | flops 2147483648 | bytes 2097152 | tf_op jit(solution)/shard_map/prefix_attend/pallas_call | solution.py:249
  55.8 26.9 %all_to_all.31 = s16[64,9,2,128]{3,2,1,0:T(2,128)(2,1)S(1)} all-to-all(s16[64,9,2,128]{3,2,1,0:T(2,128)(2,1)S(1)} %bitcast.14), channel_id=1, replica_groups=mesh['prefix'=64,'tensor'=8] {'prefix'}, dimensions={0} | all-to-all | bytes 589824 | tf_op jit(solution)/shard_map/all_to_all | solution.py:361
  82.7 1.2 %combine.1 = bf16[8,8,1024]{2,1,0:T(8,128)(2,1)S(1)} custom-call(s32[256]{0:T(256)S(1)} %pad.4.table_in_ref, s16[1152,128]{1,0:T(8,128)(2,1)S(1)} %bitcast.12, f32[64,8,128]{2,1,0:T(8,128)S(1)} %get-tuple-element.15.part_ref, f32[64,8,128]{2,1,0:T(8,128)S(1)} %get-tuple-element.16.lse_ref), custom_call_target="tpu_custom_call" | custom-call | tf_op jit(solution)/shard_map/combine/pallas_call | solution.py:318
  83.9 12.6 %all_to_all.32 = bf16[8,8,1024]{2,1,0:T(8,128)(2,1)S(1)} all-to-all(bf16[8,8,1024]{2,1,0:T(8,128)(2,1)S(1)} %combine.1), channel_id=1, replica_groups=mesh['prefix'=64,'tensor'=8] {'tensor'}, dimensions={0} | all-to-all | bytes 262144 | tf_op jit(solution)/shard_map/all_to_all | solution.py:365
  96.5 0.7 copy.8
  (2 shorter events, 0.0 us)
Async XLA Ops:
  0.0 15.4 %all-to-all-start = ((bf16[8,8,1024]{2,0,1:T(8,128)(2,1)}), bf16[8,8,1024]{2,0,1:T(8,128)(2,1)S(1)}, u32[]{:S(2)}, u32[]{:S(2)}) async-start(bf16[8,8,1024]{2,0,1:T(8,128)(2,1)} %bitcast.17), calls=%async_computation | async-start | bytes 262144 | tf_op jit(solution)/shard_map/all_to_all | solution.py:340
  16.7 33.5 %all-to-all-start.1 = ((bf16[64,16,128]{2,1,0:T(8,128)(2,1)}), bf16[64,16,128]{2,1,0:T(8,128)(2,1)S(1)}, u32[]{:S(2)}, u32[]{:S(2)}) async-start(bf16[64,16,128]{2,1,0:T(8,128)(2,1)} %bitcast.3), calls=%async_computation.1 | async-start | bytes 524288 | tf_op jit(solution)/shard_map/all_to_all | solution.py:356
  30.9 1.6 %copy-start = (bf16[64,2,1,64,128]{4,3,2,1,0:T(8,128)(2,1)S(1)}, bf16[64,2,1,64,128]{4,3,2,1,0:T(8,128)(2,1)}, u32[]{:S(2)}) copy-start(bf16[64,2,1,64,128]{4,3,2,1,0:T(8,128)(2,1)} %param.7) | copy-start | bytes 6291460
  32.5 1.6 %copy-start.1 = (bf16[1,2,1,4096,128]{4,3,2,1,0:T(8,128)(2,1)S(1)}, bf16[1,2,1,4096,128]{4,3,2,1,0:T(8,128)(2,1)}, u32[]{:S(2)}) copy-start(bf16[1,2,1,4096,128]{4,3,2,1,0:T(8,128)(2,1)} %prefix_ref.1) | copy-start | bytes 6291460
  34.1 0.7 copy-start.2

commit v6 on v3

--- a/solution.py
+++ b/solution.py
@@ -26,6 +26,7 @@
 
 def dispatch_kernel(slot_ref, q_ref, out_ref, home_ref, tile_ref):
     tensor, rows, width = q_ref.shape
+    out_ref[...] = jnp.zeros_like(out_ref)
     for t in range(tensor):
         for h in range(GROUP):
             tile_ref[pl.ds((t * GROUP + h) * rows, rows), :] = q_ref[

time: 97.4 us -> 97.4 us (level)
  no operation moved by 1% of the time
where the time goes in v6:
time: 97.4 us; the launch traced here: 97 us
  blocking collectives  39.5 us (41%)
  starting transfers between devices  24.2 us (25%)
  waiting for transfers between devices  17.2 us (18%)
  Pallas kernels  10.6 us (11%)
  local copies, waits for them, and re-layouts  4.49 us (5%)
  other arithmetic  0.99 us (1%)
    all_to_all x1, blocking collectives, on_device(): lax.all_to_all(packed.reshape(owners, SENT // 2, 2, HD), 'prefix', split_...  26.9 us
    all_to_all x1, starting transfers between devices, on_device(): lax.all_to_all(outgoing.reshape(owners, SLOTS * GROUP, HD), 'prefix', spl...  14.1 us
    all_to_all x1, waiting for transfers between devices, on_device(): lax.all_to_all(outgoing.reshape(owners, SLOTS * GROUP, HD), 'prefix', spl...  12.9 us
    all_to_all x1, blocking collectives, on_device(): lax.all_to_all(attended, 'tensor', split_axis=0, concat_axis=0, tiled=True)  12.6 us
    all_to_all x1, starting transfers between devices, on_device(): lax.all_to_all(queries, 'tensor', split_axis=1, concat_axis=0, tiled=True)  10.1 us
    pallas_call x1, Pallas kernels, prefix_attend(): pl.pallas_call(prefix_kernel, out_shape=jax.ShapeDtypeStruct((homes * SEN...  5.53 us
    unnamed x7, local copies, waits for them, and re-layouts  4.49 us
    all_to_all x1, waiting for transfers between devices, on_device(): lax.all_to_all(queries, 'tensor', split_axis=1, concat_axis=0, tiled=True)  4.26 us
  transfers between devices with their start and end apart: 2, of which 2 were waited for; matrix products, arithmetic and copies ran while one was open for 1% of the time, Pallas kernels for 3%

profile of v6, /device:TPU:1, one launch (start us, length us, event | category | flops | bytes accessed | tf_op | source)
XLA Modules:
  0.0 97.0 jit_solution(16078335857230891987)
XLA Ops:
  0.0 10.1 %all-to-all-start = ((bf16[8,8,1024]{2,0,1:T(8,128)(2,1)}), bf16[8,8,1024]{2,0,1:T(8,128)(2,1)S(1)}, u32[]{:S(2)}, u32[]{:S(2)}) async-start(bf16[8,8,1024]{2,0,1:T(8,128)(2,1)} %bitcast.17), calls=%async_computation | async-start | bytes 262144 | tf_op jit(solution)/shard_map/all_to_all | solution.py:319
  10.1 0.9 select_reduce_fusion
  11.0 0.1 pad_add_fusion.slot_ref
  11.1 4.3 %all-to-all-done = bf16[8,8,1024]{2,0,1:T(8,128)(2,1)S(1)} async-done(((bf16[8,8,1024]{2,0,1:T(8,128)(2,1)}), bf16[8,8,1024]{2,0,1:T(8,128)(2,1)S(1)}, u32[]{:S(2)}, u32[]{:S(2)}) %all-to-all-start) | async-done | bytes 131104 | tf_op jit(solution)/shard_map/all_to_all | solution.py:319
  15.4 1.3 %dispatch.1 = (bf16[128,8,128]{2,1,0:T(8,128)(2,1)}, bf16[32,16,128]{2,1,0:T(8,128)(2,1)S(1)}) custom-call(s32[65]{0:T(128)S(1)} %pad_add_fusion.slot_ref, bf16[8,8,1024]{2,1,0:T(8,128)(2,1)S(1)} %bitcast.13), custom_call_target="tpu_custom_call" | custom-call | tf_op jit(solution)/shard_map/dispatch/pallas_call | solution.py:49
  16.7 14.1 %all-to-all-start.1 = ((bf16[64,16,128]{2,1,0:T(8,128)(2,1)}), bf16[64,16,128]{2,1,0:T(8,128)(2,1)S(1)}, u32[]{:S(2)}, u32[]{:S(2)}) async-start(bf16[64,16,128]{2,1,0:T(8,128)(2,1)} %bitcast.3), calls=%async_computation.1 | async-start | bytes 524288 | tf_op jit(solution)/shard_map/all_to_all | solution.py:331
  30.8 0.0 copy-start
  30.8 1.6 %copy-done = bf16[64,2,1,64,128]{4,3,2,1,0:T(8,128)(2,1)S(1)} copy-done((bf16[64,2,1,64,128]{4,3,2,1,0:T(8,128)(2,1)S(1)}, bf16[64,2,1,64,128]{4,3,2,1,0:T(8,128)(2,1)}, u32[]{:S(2)}) %copy-start) | copy-done | bytes 2097176
  32.4 0.0 copy-start.1
  32.4 1.6 %copy-done.1 = bf16[1,2,1,4096,128]{4,3,2,1,0:T(8,128)(2,1)S(1)} copy-done((bf16[1,2,1,4096,128]{4,3,2,1,0:T(8,128)(2,1)S(1)}, bf16[1,2,1,4096,128]{4,3,2,1,0:T(8,128)(2,1)}, u32[]{:S(2)}) %copy-start.1) | copy-done | bytes 2097176
  34.0 0.0 copy-start.2
  34.0 0.7 copy-done.2
  34.7 2.6 %suffix_attend.1 = (f32[64,8,128]{2,1,0:T(8,128)S(1)}, f32[64,8,128]{2,1,0:T(8,128)S(1)}, bf16[4096,128]{1,0:T(8,128)(2,1)S(1)}, bf16[32,128,128]{2,1,0:T(8,128)(2,1)S(1)}) custom-call(s32[64]{0:T(128)S(1)} %copy-done.2, bf16[32,16,128]{2,1,0:T(8,128)(2,1)S(1)} %get-tuple-element.12.q_ref, bf16[64,2,64,128]{3,2,1,0:T(8,128)(2,1)S(1)} %bitcast.11, ...), custom_call_target="tpu_custom_call" | custom-call | flops 16777216 | bytes 4194304 | tf_op jit(solution)/shard_map/suffix_attend/pallas_call | solution.py:122
  37.3 12.9 %all-to-all-done.1 = bf16[64,16,128]{2,1,0:T(8,128)(2,1)S(1)} async-done(((bf16[64,16,128]{2,1,0:T(8,128)(2,1)}), bf16[64,16,128]{2,1,0:T(8,128)(2,1)S(1)}, u32[]{:S(2)}, u32[]{:S(2)}) %all-to-all-start.1) | async-done | bytes 262176 | tf_op jit(solution)/shard_map/all_to_all | solution.py:331
  50.2 5.5 %prefix_attend.1 = s16[1152,128]{1,0:T(8,128)(2,1)S(1)} custom-call(bf16[1024,128]{1,0:T(8,128)(2,1)S(1)} %bitcast.15, bf16[4096,128]{1,0:T(8,128)(2,1)S(1)} %get-tuple-element.13.k_ref, bf16[32,128,128]{2,1,0:T(8,128)(2,1)S(1)} %get-tuple-element.14.vt_ref), custom_call_target="tpu_custom_call" | custom-call | flops 2147483648 | bytes 2097152 | tf_op jit(solution)/shard_map/prefix_attend/pallas_call | solution.py:232
  55.8 26.9 %all_to_all.31 = s16[64,9,2,128]{3,2,1,0:T(2,128)(2,1)S(1)} all-to-all(s16[64,9,2,128]{3,2,1,0:T(2,128)(2,1)S(1)} %bitcast.14), channel_id=1, replica_groups=mesh['prefix'=64,'tensor'=8] {'prefix'}, dimensions={0} | all-to-all | bytes 589824 | tf_op jit(solution)/shard_map/all_to_all | solution.py:336
  82.7 1.1 %combine.1 = bf16[8,8,1024]{2,1,0:T(8,128)(2,1)S(1)} custom-call(s32[65]{0:T(128)S(1)} %pad_add_fusion.slot_ref, s16[1152,128]{1,0:T(8,128)(2,1)S(1)} %bitcast.12, f32[64,8,128]{2,1,0:T(8,128)S(1)} %get-tuple-element.15.part_ref, f32[64,8,128]{2,1,0:T(8,128)S(1)} %get-tuple-element.16.lse_ref), custom_call_target="tpu_custom_call" | custom-call | tf_op jit(solution)/shard_map/combine/pallas_call | solution.py:299
  83.8 12.6 %all_to_all.32 = bf16[8,8,1024]{2,1,0:T(8,128)(2,1)S(1)} all-to-all(bf16[8,8,1024]{2,1,0:T(8,128)(2,1)S(1)} %combine.1), channel_id=1, replica_groups=mesh['prefix'=64,'tensor'=8] {'tensor'}, dimensions={0} | all-to-all | bytes 262144 | tf_op jit(solution)/shard_map/all_to_all | solution.py:340
  96.4 0.7 copy.8
  (1 shorter events, 0.0 us)
Async XLA Ops:
  0.0 15.4 %all-to-all-start = ((bf16[8,8,1024]{2,0,1:T(8,128)(2,1)}), bf16[8,8,1024]{2,0,1:T(8,128)(2,1)S(1)}, u32[]{:S(2)}, u32[]{:S(2)}) async-start(bf16[8,8,1024]{2,0,1:T(8,128)(2,1)} %bitcast.17), calls=%async_computation | async-start | bytes 262144 | tf_op jit(solution)/shard_map/all_to_all | solution.py:319
  16.7 33.5 %all-to-all-start.1 = ((bf16[64,16,128]{2,1,0:T(8,128)(2,1)}), bf16[64,16,128]{2,1,0:T(8,128)(2,1)S(1)}, u32[]{:S(2)}, u32[]{:S(2)}) async-start(bf16[64,16,128]{2,1,0:T(8,128)(2,1)} %bitcast.3), calls=%async_computation.1 | async-start | bytes 524288 | tf_op jit(solution)/shard_map/all_to_all | solution.py:331
  30.8 1.6 %copy-start = (bf16[64,2,1,64,128]{4,3,2,1,0:T(8,128)(2,1)S(1)}, bf16[64,2,1,64,128]{4,3,2,1,0:T(8,128)(2,1)}, u32[]{:S(2)}) copy-start(bf16[64,2,1,64,128]{4,3,2,1,0:T(8,128)(2,1)} %param.7) | copy-start | bytes 6291460
  32.4 1.6 %copy-start.1 = (bf16[1,2,1,4096,128]{4,3,2,1,0:T(8,128)(2,1)S(1)}, bf16[1,2,1,4096,128]{4,3,2,1,0:T(8,128)(2,1)}, u32[]{:S(2)}) copy-start(bf16[1,2,1,4096,128]{4,3,2,1,0:T(8,128)(2,1)} %prefix_ref.1) | copy-start | bytes 6291460
  34.0 0.7 copy-start.2
